TPU v7x, 128 devices: a whole 4x4x4 slice. The times are simulated.
128 devices in a mesh: rep: 4 (over y), ep: 32 (over z, x, core).
Axes of the slice: x: 4, y: 4, z: 4, core: 2. Of those that a mesh axis runs over, the one named last changes fastest.
Arguments:
- tokens: bfloat16 [16384, 2048], P(('rep', 'ep')), may hold values from -6 to 6
- expert_ids: int32 [16384, 6], P(('rep', 'ep')), may hold values from 0 to 31, all different within a row; in each aligned block of 128 rows (0 to 127, 128 to 255, ...) at most 32 rows name the same one
- gate_weights: float32 [16384, 6], P(('rep', 'ep')), may hold values from 0.03 to 0.5
- cotangent: bfloat16 [16384, 2048], P(('rep', 'ep')), may hold values from -4 to 4
- w_gate: bfloat16 [32, 2048, 704], P('ep'), may hold values from -0.125 to 0.125
- w_up: bfloat16 [32, 2048, 704], P('ep'), may hold values from -0.125 to 0.125
- w_down: bfloat16 [32, 704, 2048], P('ep'), may hold values from -0.21875 to 0.21875
Outputs:
- mixed: bfloat16 [16384, 2048], P(('rep', 'ep'))
- token_grad: bfloat16 [16384, 2048], P(('rep', 'ep'))
- gate_grad: float32 [16384, 6], P(('rep', 'ep'))
- grad_w_gate: float32 [32, 2048, 704], P('ep', 'rep')
- grad_w_up: float32 [32, 2048, 704], P('ep', 'rep')
- grad_w_down: float32 [32, 704, 2048], P('ep', 'rep')
Inputs may be any that keep to these rules, and one draw needn't show every extreme that they name: `expert_ids`: A token's 6 expert ids are distinct; among the tokens of one device no expert is named by more than 32 choices.
All inputs are finite; a program needn't handle non-finite values.
Results may differ from a plain program's by a relative error of at most 0.0085.
Values may be sent and summed in bfloat16 or wider, within the bound.
No kernel may reach another device: no remote copies, remote signals or barrier semaphores. Data moves between devices by JAX's collectives and lax.ppermute only.
A program may use at most 128 MiB of HBM per device.

v0:
```python
import functools

import jax
import jax.numpy as jnp
from jax import lax
from jax.experimental import pallas as pl
from jax.experimental.pallas import tpu as pltpu
from jax.sharding import PartitionSpec as P


F32 = jnp.float32
BF16 = jnp.bfloat16
SIDE = 4
CORES = 2
LANES = 128
CAP = 32
TOP = 6
DESTS = SIDE * CORES
TILE = 512
WIDE = 1024
ROWS = SIDE * CAP


def device_of(z, x, c):
    return (z % SIDE) * SIDE * CORES + (x % SIDE) * CORES + c


def shift_pairs(axis, step, flip):
    pairs = []
    for z in range(SIDE):
        for x in range(SIDE):
            for c in range(CORES):
                there = device_of(z, x + step, c ^ flip) if axis == "x" else device_of(z + step, x, c ^ flip)
                pairs.append((device_of(z, x, c), there))
    return pairs


def move(value, axis, step, flip=0):
    if step % SIDE == 0 and flip == 0:
        return value
    return lax.ppermute(value, "ep", shift_pairs(axis, step, flip))


def position():
    at = lax.axis_index("ep")
    return at >> 3, (at >> 1) & 3, at & 1


def local_experts(axis, offset=0):
    z, x, c = position()
    q = lax.broadcasted_iota(jnp.int32, (DESTS, LANES), 0)
    k, flip = q >> 1, q & 1
    core = (c + flip) & 1
    if axis == "x":
        ids = (z << 3) + (((x + k) & 3) << 1) + core
    else:
        ids = (((z + k) & 3) << 3) + (((x + offset) & 3) << 1) + core
    return ids.astype(F32)


def thirds(value):
    high = value.astype(BF16)
    rest = value - high.astype(F32)
    mid = rest.astype(BF16)
    return high, mid, (rest - mid.astype(F32)).astype(BF16)


def stage_body(tokens, cot, ids, weights, tokens_out, cot_out, meta_out):
    tokens_out[...] = tokens[...]
    cot_out[...] = cot[...]
    meta_out[...] = jnp.zeros(meta_out.shape, F32)
    meta_out[0:TOP, :] = ids[...].astype(F32)
    meta_out[8 : 8 + TOP, :] = weights[...]


def stack_body(gate_t, up_t, both_out):
    both_out[0] = gate_t[...]
    both_out[1] = up_t[...]


def selection(meta, experts):
    ids, gate = meta[0:TOP, :], meta[8 : 8 + TOP, :]
    named = jnp.zeros((DESTS, LANES), F32)
    weight = jnp.zeros((DESTS, LANES), F32)
    for j in range(TOP):
        hit = ids[j : j + 1, :] == experts
        named = named + jnp.where(hit, 1.0, 0.0)
        weight = weight + jnp.where(hit, gate[j : j + 1, :], 0.0)
    earlier = lax.broadcasted_iota(jnp.int32, (LANES, LANES), 0) < lax.broadcasted_iota(
        jnp.int32, (LANES, LANES), 1
    )
    before = jnp.dot(
        named.astype(BF16), jnp.where(earlier, 1.0, 0.0).astype(BF16), preferred_element_type=F32
    )
    place = jnp.where(named > 0.5, before, -1.0)
    slot = lax.broadcasted_iota(jnp.int32, (CAP, LANES), 0).astype(F32)
    chosen = jnp.concatenate(
        [
            jnp.where(jnp.broadcast_to(place[q : q + 1, :], (CAP, LANES)) == slot, 1.0, 0.0)
            for q in range(DESTS)
        ],
        axis=0,
    )
    spread = jnp.concatenate(
        [jnp.broadcast_to(weight[q : q + 1, :], (CAP, LANES)) for q in range(DESTS)], axis=0
    )
    return chosen, spread


def dispatch_body(axis, scaled, *refs):
    sources, metas, outs = refs[:4], refs[4:8], refs[8:]
    experts = local_experts(axis)
    for s in range(SIDE):
        chosen, spread = selection(metas[s], experts)
        scale = jnp.sum(chosen * spread, axis=1, keepdims=True) if scaled else None
        chosen = chosen.astype(BF16)

        def column(n, carry, s=s, chosen=chosen, scale=scale):
            at = pl.ds(pl.multiple_of(n * WIDE, WIDE), WIDE)
            rows = jnp.dot(chosen, sources[s][:, at], preferred_element_type=F32)
            if scaled:
                rows = rows * scale
            rows = rows.astype(BF16)
            for q in range(DESTS):
                outs[q][s * CAP : (s + 1) * CAP, at] = rows[q * CAP : (q + 1) * CAP, :]
            return carry

        lax.fori_loop(0, outs[0].shape[1] // WIDE, column, 0)


def contract_rows(left, right):
    return lax.dot_general(left, right, (((0,), (0,)), ((), ())), preferred_element_type=F32)


def contract_lanes(left, right):
    return lax.dot_general(left, right, (((1,), (1,)), ((), ())), preferred_element_type=F32)


def source_rows(blocks, s, columns):
    return jnp.concatenate(
        [blocks[q][s * CAP : (s + 1) * CAP, columns] for q in range(DESTS)], axis=0
    )


def combine_out_body(*refs):
    blocks, metas, outs = refs[:8], refs[8:12], refs[12:]
    experts = local_experts("x")
    for s in range(SIDE):
        chosen, spread = selection(metas[s], experts)
        mix = chosen * spread
        high = mix.astype(BF16)
        mix = jnp.concatenate([high, (mix - high.astype(F32)).astype(BF16)], axis=1)

        def column(n, carry, s=s, mix=mix):
            at = pl.ds(pl.multiple_of(n * TILE, TILE), TILE)
            both = contract_rows(mix, source_rows(blocks, s, at))
            outs[s][:, at] = (both[:LANES, :] + both[LANES:, :]).astype(BF16)
            return carry

        lax.fori_loop(0, outs[0].shape[1] // TILE, column, 0)


def combine_grad_body(*refs):
    blocks, metas, outs = refs[:8], refs[8:12], refs[12:]
    experts = local_experts("z")
    columns = []
    for q in range(DESTS):
        product = blocks[q][ROWS : ROWS + 8, 0 : 3 * LANES].astype(F32)
        product = (product[:, :LANES] + product[:, LANES : 2 * LANES]) + product[:, 2 * LANES :]
        columns.append(jnp.transpose(jnp.broadcast_to(product[0:1, :], (LANES, LANES))))
    for s in range(SIDE):
        chosen, _ = selection(metas[s], experts)
        picked = chosen.astype(BF16)

        def column(n, carry, s=s, picked=picked):
            at = pl.ds(pl.multiple_of(n * TILE, TILE), TILE)
            outs[s][0:LANES, at] = contract_rows(picked, source_rows(blocks, s, at)).astype(BF16)
            return carry

        width = outs[0].shape[1]
        lax.fori_loop(0, width // TILE, column, 0)
        gains = jnp.concatenate(
            [
                jnp.sum(
                    chosen[q * CAP : (q + 1) * CAP, :] * columns[q][s * CAP : (s + 1) * CAP, :],
                    axis=0,
                    keepdims=True,
                )
                for q in range(DESTS)
            ],
            axis=0,
        )
        outs[s][LANES : LANES + 8, 0 : 3 * LANES] = jnp.concatenate(thirds(gains), axis=1)
        outs[s][LANES : LANES + 8, 3 * LANES :] = jnp.zeros((8, width - 3 * LANES), BF16)


def sum_parts_body(*refs):
    parts, out = refs[:4], refs[4]
    out[...] = (
        (parts[0][...].astype(F32) + parts[1][...].astype(F32))
        + (parts[2][...].astype(F32) + parts[3][...].astype(F32))
    ).astype(BF16)


def finish_grad_body(*refs):
    parts, meta, out, gate_out = refs[:4], refs[4], refs[5], refs[6]
    sum_parts_body(*[p.at[0:LANES, :] for p in parts], out)
    ids, gate = meta[0:TOP, :], meta[8 : 8 + TOP, :]
    total = [jnp.zeros((1, LANES), F32) for _ in range(TOP)]
    for k in range(SIDE):
        experts = local_experts("z", k)
        gains = parts[k][LANES : LANES + 8, 0 : 3 * LANES].astype(F32)
        gains = (gains[:, :LANES] + gains[:, LANES : 2 * LANES]) + gains[:, 2 * LANES :]
        for j in range(TOP):
            hit = ids[j : j + 1, :] == experts
            total[j] = total[j] + jnp.sum(jnp.where(hit, gains, 0.0), axis=0, keepdims=True)
    total = [total[j] / gate[j : j + 1, :] for j in range(TOP)]
    gate_out[...] = jnp.concatenate(total, axis=0)


def forward_body(count, *refs):
    blocks, (both, down), outs = refs[:count], refs[count : count + 2], refs[count + 2 : 2 * count + 2]
    gate_factor_out, silu_out, act_out, staged, pre = refs[2 * count + 2 :]
    for i in range(count):
        staged[i * ROWS : (i + 1) * ROWS, :] = blocks[i][...]

    def part(n, carry):
        at = pl.ds(pl.multiple_of(n * 2 * ROWS, 2 * ROWS), 2 * ROWS)

        def project(i, inner):
            pre[i] = contract_lanes(staged[at, :], both[i])
            return inner

        lax.fori_loop(0, 2, project, 0)
        gate_pre, up_pre = pre[0], pre[1]
        sigmoid_val = jax.nn.sigmoid(gate_pre)
        silu_val = gate_pre * sigmoid_val
        factor = up_pre * sigmoid_val * (1.0 + gate_pre * (1.0 - sigmoid_val))
        gate_factor_out[at, :] = factor.astype(BF16)
        silu_out[at, :] = silu_val.astype(BF16)
        act_out[at, :] = (silu_val * up_pre).astype(BF16)
        return carry

    if count == 2:
        part(0, 0)
    else:
        lax.fori_loop(0, count // 2, part, 0)

    def column(n, carry):
        at = pl.ds(pl.multiple_of(n * TILE, TILE), TILE)
        result = jnp.dot(act_out[...], down[:, at], preferred_element_type=F32).astype(BF16)
        for i in range(count):
            outs[i][:, at] = result[i * ROWS : (i + 1) * ROWS, :]
        return carry

    lax.fori_loop(0, down.shape[1] // TILE, column, 0)


def hidden_slices(counts):
    place = {}
    for n, ks in enumerate(counts):
        for i, k in enumerate(ks):
            for flip in range(CORES):
                place[2 * k + flip] = (n, (2 * i + flip) * ROWS)
    return place


def backward_body(kzs, place, arrays, *refs):
    count = 2 * len(kzs)
    cots, refs = refs[:count], refs[count:]
    factors, silus, acts, refs = refs[:arrays], refs[arrays : 2 * arrays], refs[2 * arrays : 3 * arrays], refs[3 * arrays :]
    (both, down), refs = refs[:2], refs[2:]
    outs, gate_grad_out, up_grad_out = refs[:count], refs[count], refs[count + 1]

    def ordered(parts):
        pieces = []
        for kz in kzs:
            for flip in range(CORES):
                for kx in range(SIDE):
                    n, first = place[2 * kx + flip]
                    pieces.append(parts[n][first + kz * CAP : first + (kz + 1) * CAP, :])
        return jnp.concatenate(pieces, axis=0)

    cot = jnp.concatenate([c[...] for c in cots], axis=0)
    act_grad = contract_lanes(cot, down[...])
    gate_grad_out[...] = (act_grad * ordered(factors).astype(F32)).astype(BF16)
    up_grad_out[...] = (act_grad * ordered(silus).astype(F32)).astype(BF16)
    product = jnp.sum(ordered(acts).astype(F32) * act_grad, axis=1, keepdims=True)
    width = down.shape[1]
    for n in range(count):
        part = jnp.broadcast_to(product[n * ROWS : (n + 1) * ROWS, :], (ROWS, LANES))
        part = jnp.transpose(part)[0:8, :]
        outs[n][ROWS : ROWS + 8, 0 : 3 * LANES] = jnp.concatenate(thirds(part), axis=1)
        outs[n][ROWS : ROWS + 8, 3 * LANES :] = jnp.zeros((8, width - 3 * LANES), BF16)

    def column(n, carry):
        at = pl.ds(pl.multiple_of(n * TILE, TILE), TILE)
        result = (
            jnp.dot(gate_grad_out[...], both[0, :, at], preferred_element_type=F32)
            + jnp.dot(up_grad_out[...], both[1, :, at], preferred_element_type=F32)
        ).astype(BF16)
        for i in range(count):
            outs[i][0:ROWS, at] = result[i * ROWS : (i + 1) * ROWS, :]
        return carry

    lax.fori_loop(0, width // TILE, column, 0)


def in_cot_order(blocks, columns, kzs):
    return jnp.concatenate(
        [
            blocks[2 * kx + flip][kz * CAP : (kz + 1) * CAP, columns]
            for kz in kzs
            for flip in range(CORES)
            for kx in range(SIDE)
        ],
        axis=0,
    )


def column_grad_body(order, arrays, *refs):
    gates, ups, blocks = refs[:arrays], refs[arrays : 2 * arrays], refs[2 * arrays : 2 * arrays + 8]
    own, ahead, behind, ahead_kept, behind_kept, turned, piece = refs[2 * arrays + 8 :]
    rep = lax.axis_index("rep")
    width = own.shape[1]
    hidden = gates[0].shape[1]
    turned[0] = jnp.transpose(jnp.concatenate([h[...] for h in gates], axis=0))
    turned[1] = jnp.transpose(jnp.concatenate([h[...] for h in ups], axis=0))
    places = ((own.at[0:hidden, :], own.at[hidden:, :]), (ahead_kept, ahead.at[0:hidden, :]),
              (ahead.at[hidden:, :], behind.at[hidden:, :]), (behind.at[0:hidden, :], behind_kept))

    def chunk(k, carry):
        start = pl.multiple_of(((rep + k) & 3) * width, LANES)
        right = in_cot_order(blocks, pl.ds(start, width), order)
        for half in range(2):
            piece[half] = jnp.dot(turned[half], right, preferred_element_type=F32).astype(BF16)
        for n in range(4):

            @pl.when(k == n)
            def _():
                for half in range(2):
                    places[n][half][...] = piece[half]

        return carry

    lax.fori_loop(0, 4, chunk, 0)


def row_grad_body(place, arrays, *refs):
    acts, blocks = refs[:arrays], refs[arrays : arrays + 8]
    own, ahead, behind, ahead_kept, behind_kept, turned, whole = refs[arrays + 8 :]
    rep = lax.axis_index("rep")
    height, width = own.shape
    half = width // 2
    pieces = []
    for kz in range(SIDE):
        for flip in range(CORES):
            for kx in range(SIDE):
                n, first = place[2 * kx + flip]
                pieces.append(acts[n][first + kz * CAP : first + (kz + 1) * CAP, :])
    turned[...] = jnp.transpose(jnp.concatenate(pieces, axis=0))

    def column(n, carry):
        at = pl.ds(pl.multiple_of(n * TILE, TILE), TILE)
        right = jnp.concatenate([b[:, at] for b in blocks], axis=0)
        whole[:, at] = jnp.dot(turned[...], right, preferred_element_type=F32).astype(BF16)
        return carry

    lax.fori_loop(0, width // TILE, column, 0)

    def rows_for(k):
        return pl.ds(pl.multiple_of(((rep + k) & 3) * height, 16), height)

    own[...] = whole[rows_for(0), :]
    ahead_kept[...] = whole[rows_for(1), 0:half]
    ahead[:, 0:half] = whole[rows_for(1), half:]
    ahead[:, half:] = whole[rows_for(2), 0:half]
    behind[:, 0:half] = whole[rows_for(3), 0:half]
    behind[:, half:] = whole[rows_for(2), half:]
    behind_kept[...] = whole[rows_for(3), half:]


def relay_body(axis, from_behind, from_ahead, ahead_kept, behind_kept, ahead_out, behind_out):
    far = slice(ahead_kept.shape[axis], None)
    at = (far, slice(None)) if axis == 0 else (slice(None), far)
    ahead_out[...] = (from_behind[at].astype(F32) + ahead_kept[...].astype(F32)).astype(BF16)
    behind_out[...] = (from_ahead[at].astype(F32) + behind_kept[...].astype(F32)).astype(BF16)


def call(body, args, outs, flops, scratch=(), limit=14):
    moved = sum(a.size * a.dtype.itemsize for a in args) + sum(
        o.size * o.dtype.itemsize for o in outs
    )
    vmem = pl.BlockSpec(memory_space=pltpu.VMEM)
    return pl.pallas_call(
        body,
        out_shape=tuple(outs),
        in_specs=[vmem] * len(args),
        out_specs=tuple([vmem] * len(outs)),
        scratch_shapes=list(scratch),
        cost_estimate=pl.CostEstimate(flops=flops, bytes_accessed=moved, transcendentals=0),
        compiler_params=pltpu.CompilerParams(vmem_limit_bytes=limit * 1024 * 1024),
    )(*args)


def per_device(tokens, expert_ids, gate_weights, cotangent, w_gate, w_up, w_down):
    tok_rows, width = tokens.shape
    gate_t = jnp.swapaxes(w_gate[0], 0, 1)
    up_t = jnp.swapaxes(w_up[0], 0, 1)
    down = w_down[0]
    hidden = down.shape[0]

    def block(dtype=BF16, rows=ROWS, columns=width):
        return jax.ShapeDtypeStruct((rows, columns), dtype)

    tall = block(BF16, ROWS + 8)
    own_tokens, own_cot, meta = call(
        stage_body, [tokens, cotangent, expert_ids.T, gate_weights.T],
        [block(), block(), block(F32, 16, tok_rows)], 0, limit=4,
    )
    (both,) = call(
        stack_body, [gate_t, up_t], [jax.ShapeDtypeStruct((2, hidden, width), BF16)], 0,
        limit=14,
    )
    hops = (1, 3, 2)
    token_parts, cot_parts = {0: own_tokens}, {0: own_cot}
    meta_z, meta_x = {0: meta}, {0: meta}
    for k in hops:
        token_parts[k] = move(tokens, "z", k, 0)
        cot_parts[k] = move(cotangent, "x", k, 0)
        meta_z[k] = move(meta, "z", k, 0)
        meta_x[k] = move(meta, "x", k, 0)

    def four(parts):
        return [parts[k] for k in range(SIDE)]

    from_z, from_x = four(token_parts) + four(meta_z), four(cot_parts) + four(meta_x)
    gather_flops = 2 * DESTS * ROWS * LANES * width
    sent = call(
        functools.partial(dispatch_body, "x", False), from_z, [block()] * DESTS, gather_flops,
        limit=10,
    )
    sent_cot = call(
        functools.partial(dispatch_body, "z", True), from_x, [block()] * DESTS, gather_flops,
        limit=10,
    )
    rows = [move(sent[q], "x", q >> 1, q & 1) for q in range(DESTS)]
    cots = [move(sent_cot[q], "z", q >> 1, q & 1) for q in range(DESTS)]

    unit = 2 * ROWS * width * hidden
    groups = ((0, 1), (2, 3))
    place = hidden_slices(groups)
    out_blocks, gates, ups, acts = {}, [], [], []
    for ks in groups:
        qs = [2 * k + flip for k in ks for flip in range(CORES)]
        count = len(qs)
        results = call(
            functools.partial(forward_body, count),
            [rows[q] for q in qs] + [both, down],
            [block()] * count + [block(BF16, count * ROWS, hidden)] * 3,
            3 * count * unit, [pltpu.VMEM((count * ROWS, width), BF16), pltpu.VMEM((2, 2 * ROWS, hidden), F32)],
            limit=10,
        )
        for q, value in zip(qs, results):
            out_blocks[q] = value
        gates.append(results[count])
        ups.append(results[count + 1])
        acts.append(results[count + 2])
    out_back = [move(out_blocks[q], "x", -(q >> 1), q & 1) for q in range(DESTS)]

    back_groups = ((1, 3), (2, 0))
    row_blocks, gate_grads, up_grads = {}, [], []
    for ks in back_groups:
        qs = [2 * k + flip for k in ks for flip in range(CORES)]
        count = len(qs)
        results = call(
            functools.partial(backward_body, ks, place, len(groups)),
            [cots[q] for q in qs] + gates + ups + acts + [both, down],
            [tall] * count + [block(BF16, count * ROWS, hidden)] * 2,
            3 * count * unit, limit=11,
        )
        for q, value in zip(qs, results):
            row_blocks[q] = value
        gate_grads.append(results[count])
        up_grads.append(results[count + 1])
    rows_back = [move(row_blocks[q], "z", -(q >> 1), q & 1) for q in range(DESTS)]

    order = tuple(k for ks in back_groups for k in ks)

    def chunks(rows_, columns, axis):
        halved = (rows_ // 2, columns) if axis == 0 else (rows_, columns // 2)
        return [block(BF16, rows_, columns)] * 3 + [block(BF16, *halved)] * 2

    down_parts = call(
        functools.partial(row_grad_body, place, len(groups)), acts + cots,
        chunks(hidden // 4, width, 1), 8 * unit,
        [pltpu.VMEM((hidden, DESTS * ROWS), BF16), pltpu.VMEM((hidden, width), BF16)],
    )
    both_parts = call(
        functools.partial(column_grad_body, order, len(back_groups)),
        gate_grads + up_grads + rows, chunks(2 * hidden, width // 4, 0), 16 * unit,
        [pltpu.VMEM((2, hidden, DESTS * ROWS), BF16), pltpu.VMEM((2, hidden, width // 4), BF16)],
    )

    def pass_on(value, step):
        return lax.ppermute(value, "rep", [(r, (r + step) % 4) for r in range(4)])

    def reduced(parts, axis):
        own, ahead, behind, ahead_kept, behind_kept = parts
        from_behind = pass_on(ahead, 1)
        from_ahead = pass_on(behind, 3)
        ahead, behind = call(
            functools.partial(relay_body, axis),
            [from_behind, from_ahead, ahead_kept, behind_kept],
            [jax.ShapeDtypeStruct(ahead_kept.shape, BF16)] * 2, ahead_kept.size,
            limit=8,
        )
        relayed_behind = pass_on(ahead, 1)
        relayed_ahead = pass_on(behind, 3)

        def halves(value):
            return [h.astype(F32) for h in jnp.split(value, 2, axis=axis)]

        (own_a, own_b), near_b, near_a = halves(own), halves(from_behind)[0], halves(from_ahead)[0]
        return (
            own_a + near_a + relayed_behind.astype(F32), own_b + near_b + relayed_ahead.astype(F32)
        )

    grad_down = jnp.concatenate(reduced(down_parts, 1), axis=1)[None]
    grad_gate, grad_up = [jnp.swapaxes(g, 0, 1)[None] for g in reduced(both_parts, 0)]

    mixed_parts = call(
        combine_out_body, out_back + from_z[4:], [block()] * SIDE, 2 * gather_flops,
        limit=10,
    )
    mixed_parts = [move(mixed_parts[s], "z", -s, 0) for s in range(SIDE)]
    (mixed,) = call(sum_parts_body, mixed_parts, [block()], 4 * tok_rows * width, limit=4)

    grad_parts = call(
        combine_grad_body, rows_back + from_x[4:], [tall] * SIDE, gather_flops, limit=10,
    )
    grad_parts = [move(grad_parts[s], "x", -s, 0) for s in range(SIDE)]
    token_grad, gate_grad = call(
        finish_grad_body, grad_parts + [meta],
        [block(), block(F32, TOP, LANES)], 4 * tok_rows * width, limit=8,
    )
    return (mixed, token_grad, gate_grad.T, grad_gate, grad_up, grad_down)


def solution(mesh):
    placed = (
        P(("rep", "ep"), None),
        P(("rep", "ep"), None),
        P(("rep", "ep"), None),
        P(("rep", "ep"), None),
        P("ep", None, None),
        P("ep", None, None),
        P("ep", None, None),
    )

    return jax.shard_map(
        per_device,
        mesh=mesh,
        in_specs=placed,
        out_specs=(
            P(("rep", "ep"), None),
            P(("rep", "ep"), None),
            P(("rep", "ep"), None),
            P("ep", "rep", None),
            P("ep", "rep", None),
            P("ep", "rep", None),
        ),
        check_vma=False,
    )
```

profile of v0, /device:TPU:0, one launch (start us, length us, event | category | flops | bytes accessed | tf_op | source)
XLA Modules:
  0.0 306.4 jit_solution(2904712915143809983)
XLA Ops:
  12.5 15.5 %collective-permute-done.5.refs_7_.refs_11_ = f32[16,128]{1,0:T(8,128)S(1)} collective-permute-done((f32[16,128]{1,0:T(8,128)S(1)}, f32[16,128]{1,0:T(8,128)S(1)}, u32[]{:S(2)}, u32[]{:S(2)}) %collective-permute-start.5) | collective-permute-done | bytes 8224 | tf_op jit(solution)/shard_map/ppermute | solution.py:41
  28.0 3.4 %collective-permute-start.4 = (f32[16,128]{1,0:T(8,128)S(1)}, f32[16,128]{1,0:T(8,128)S(1)}, u32[]{:S(2)}, u32[]{:S(2)}) collective-permute-start(f32[16,128]{1,0:T(8,128)S(1)} %get-tuple-element.76.refs_4_.refs_8_), channel_id=1, source_target_pairs={{0,16},{1,17},{2,18},{3,19},{4,20},{5,21},{6,22},{7,23},{8,24},{9,... | collective-permute-start | bytes 24584 | tf_op jit(solution)/shard_map/ppermute | solution.py:41
  33.9 4.3 %collective-permute-done.3.refs_5_.refs_9_ = f32[16,128]{1,0:T(8,128)S(1)} collective-permute-done((f32[16,128]{1,0:T(8,128)S(1)}, f32[16,128]{1,0:T(8,128)S(1)}, u32[]{:S(2)}, u32[]{:S(2)}) %collective-permute-start.3) | collective-permute-done | bytes 8224 | tf_op jit(solution)/shard_map/ppermute | solution.py:41
  45.8 14.6 %collective-permute-done.28.refs_7_.refs_11_ = f32[16,128]{1,0:T(8,128)S(1)} collective-permute-done((f32[16,128]{1,0:T(8,128)S(1)}, f32[16,128]{1,0:T(8,128)S(1)}, u32[]{:S(2)}, u32[]{:S(2)}) %collective-permute-start.28) | collective-permute-done | bytes 8224 | tf_op jit(solution)/shard_map/ppermute | solution.py:41
  66.6 4.4 %collective-permute-done.26.refs_5_.refs_9_ = f32[16,128]{1,0:T(8,128)S(1)} collective-permute-done((f32[16,128]{1,0:T(8,128)S(1)}, f32[16,128]{1,0:T(8,128)S(1)}, u32[]{:S(2)}, u32[]{:S(2)}) %collective-permute-start.26) | collective-permute-done | bytes 8224 | tf_op jit(solution)/shard_map/ppermute | solution.py:41
  71.0 3.5 %collective-permute-start.12 = (bf16[128,2048]{1,0:T(8,128)(2,1)S(1)}, bf16[128,2048]{1,0:T(8,128)(2,1)S(1)}, u32[]{:S(2)}, u32[]{:S(2)}) collective-permute-start(bf16[128,2048]{1,0:T(8,128)(2,1)S(1)} %get-tuple-element.85), channel_id=1, source_target_pairs={{0,4},{1,5},{2,6},{3,7},{4,0},{5,1},{6,2},{7,3},{8,12},{9,13},{10,... | collective-permute-start | bytes 1572872 | tf_op jit(solution)/shard_map/ppermute | solution.py:41
  80.5 6.0 %collective-permute-done.7.refs_2_.refs_6_ = bf16[128,2048]{1,0:T(8,128)(2,1)S(1)} collective-permute-done((bf16[128,2048]{1,0:T(8,128)(2,1)S(1)}, bf16[128,2048]{1,0:T(8,128)(2,1)S(1)}, u32[]{:S(2)}, u32[]{:S(2)}) %collective-permute-start.7) | collective-permute-done | bytes 524320 | tf_op jit(solution)/shard_map/ppermute | solution.py:41
  86.4 7.6 %collective-permute-done.8.refs_3_.refs_7_ = bf16[128,2048]{1,0:T(8,128)(2,1)S(1)} collective-permute-done((bf16[128,2048]{1,0:T(8,128)(2,1)S(1)}, bf16[128,2048]{1,0:T(8,128)(2,1)S(1)}, u32[]{:S(2)}, u32[]{:S(2)}) %collective-permute-start.8) | collective-permute-done | bytes 524320 | tf_op jit(solution)/shard_map/ppermute | solution.py:41
  96.1 12.8 %collective-permute-done.12.refs_0_.refs_8_ = bf16[128,2048]{1,0:T(8,128)(2,1)S(1)} collective-permute-done((bf16[128,2048]{1,0:T(8,128)(2,1)S(1)}, bf16[128,2048]{1,0:T(8,128)(2,1)S(1)}, u32[]{:S(2)}, u32[]{:S(2)}) %collective-permute-start.12) | collective-permute-done | bytes 524320 | tf_op jit(solution)/shard_map/ppermute | solution.py:41
  111.4 4.0 %collective-permute-start.31 = (bf16[128,2048]{1,0:T(8,128)(2,1)S(1)}, bf16[128,2048]{1,0:T(8,128)(2,1)S(1)}, u32[]{:S(2)}, u32[]{:S(2)}) collective-permute-start(bf16[128,2048]{1,0:T(8,128)(2,1)S(1)} %get-tuple-element.101), channel_id=1, source_target_pairs={{0,1},{1,0},{2,3},{3,2},{4,5},{5,4},{6,7},{7,6},{8,9},{9,8},{10,11... | collective-permute-start | bytes 1572872 | tf_op jit(solution)/shard_map/ppermute | solution.py:41
  120.3 3.5 %collective-permute-start.35 = (bf16[128,2048]{1,0:T(8,128)(2,1)S(1)}, bf16[128,2048]{1,0:T(8,128)(2,1)S(1)}, u32[]{:S(2)}, u32[]{:S(2)}) collective-permute-start(bf16[128,2048]{1,0:T(8,128)(2,1)S(1)} %get-tuple-element.112), channel_id=1, source_target_pairs={{0,24},{1,25},{2,26},{3,27},{4,28},{5,29},{6,30},{7,31},{8,0},{9,1... | collective-permute-start | bytes 1572872 | tf_op jit(solution)/shard_map/ppermute | solution.py:41
  123.7 7.2 %shard_map.122 = (bf16[128,2048]{1,0:T(8,128)(2,1)S(1)}, bf16[128,2048]{1,0:T(8,128)(2,1)S(1)}, bf16[128,2048]{1,0:T(8,128)(2,1)S(1)}, bf16[128,2048]{1,0:T(8,12...) custom-call(bf16[128,2048]{1,0:T(8,128)(2,1)S(1)} %collective-permute-done.12., ...), custom_call_target="tpu_custom_call" | custom-call | flops 4429185024 | bytes 15007744 | tf_op jit(solution)/shard_map/pallas_call | solution.py:395
  135.1 11.1 %collective-permute-done.34.refs_1_.refs_5_ = bf16[128,2048]{1,0:T(8,128)(2,1)S(1)} collective-permute-done((bf16[128,2048]{1,0:T(8,128)(2,1)S(1)}, bf16[128,2048]{1,0:T(8,128)(2,1)S(1)}, u32[]{:S(2)}, u32[]{:S(2)}) %collective-permute-start.34) | collective-permute-done | bytes 524320 | tf_op jit(solution)/shard_map/ppermute | solution.py:41
  146.1 7.2 %shard_map.121 = (bf16[128,2048]{1,0:T(8,128)(2,1)S(1)}, bf16[128,2048]{1,0:T(8,128)(2,1)S(1)}, bf16[128,2048]{1,0:T(8,128)(2,1)S(1)}, bf16[128,2048]{1,0:T(8,12...) custom-call(bf16[128,2048]{1,0:T(8,128)(2,1)S(1)} %get-tuple-element.77.refs_0, ...), custom_call_target="tpu_custom_call" | custom-call | flops 4429185024 | bytes 15007744 | tf_op jit(solution)/shard_map/pallas_call | solution.py:395
  156.9 3.8 %collective-permute-start.11 = (bf16[128,2048]{1,0:T(8,128)(2,1)S(1)}, bf16[128,2048]{1,0:T(8,128)(2,1)S(1)}, u32[]{:S(2)}, u32[]{:S(2)}) collective-permute-start(bf16[128,2048]{1,0:T(8,128)(2,1)S(1)} %get-tuple-element.84), channel_id=1, source_target_pairs={{0,7},{1,6},{2,1},{3,0},{4,3},{5,2},{6,5},{7,4},{8,15},{9,14},{10,... | collective-permute-start | bytes 1572872 | tf_op jit(solution)/shard_map/ppermute | solution.py:41
  160.7 6.2 %shard_map.127 = (bf16[136,2048]{1,0:T(8,128)(2,1)S(1)}, bf16[136,2048]{1,0:T(8,128)(2,1)S(1)}, bf16[136,2048]{1,0:T(8,128)(2,1)S(1)}, bf16[136,2048]{1,0:T(8,12...) custom-call(bf16[128,2048]{1,0:T(8,128)(2,1)S(1)} %collective-permute-done.33.refs_0_.refs_4_, ...), custom_call_target="tpu_custom_call" | custom-call | flops 4429185024 | bytes 18743296 | tf_op jit(solution)/shard_map/pallas_call | solution.py:395
  170.1 10.0 %collective-permute-done.19.refs_7_ = bf16[128,2048]{1,0:T(8,128)(2,1)S(1)} collective-permute-done((bf16[128,2048]{1,0:T(8,128)(2,1)S(1)}, bf16[128,2048]{1,0:T(8,128)(2,1)S(1)}, u32[]{:S(2)}, u32[]{:S(2)}) %collective-permute-start.19) | collective-permute-done | bytes 524320 | tf_op jit(solution)/shard_map/ppermute | solution.py:41
  181.0 6.2 %shard_map.126 = (bf16[136,2048]{1,0:T(8,128)(2,1)S(1)}, bf16[136,2048]{1,0:T(8,128)(2,1)S(1)}, bf16[136,2048]{1,0:T(8,128)(2,1)S(1)}, bf16[136,2048]{1,0:T(8,12...) custom-call(bf16[128,2048]{1,0:T(8,128)(2,1)S(1)} %collective-permute-done.29.refs_0_.refs_6_, ...), custom_call_target="tpu_custom_call" | custom-call | flops 4429185024 | bytes 18743296 | tf_op jit(solution)/shard_map/pallas_call | solution.py:395
  189.9 7.9 %shard_map.130 = (bf16[1408,512]{1,0:T(8,128)(2,1)S(1)}, bf16[1408,512]{1,0:T(8,128)(2,1)S(1)}, bf16[1408,512]{1,0:T(8,128)(2,1)S(1)}, bf16[704,512]{1,0:T(8,128)(2,1)S(1)}, bf16[704,512]{1,0:T(8,128)(2,1)S(1)}) custom-call(bf16[512,704]{1,0:T(8,128)(2,1)S(1)} %get-tuple-element.126.refs_0_, bf16[512,704]{1,0:T(8,128)(2,1)S(1)} %get-tuple-element.127.refs_1_, ...), custom_call_target="tpu_custom_call" | custom-call | flops 5905580032 | bytes 12845056 | tf_op jit(solution)/shard_map/pallas_call | solution.py:395
  205.3 4.3 %shard_map.132 = (bf16[176,2048]{1,0:T(8,128)(2,1)S(1)}, bf16[176,2048]{1,0:T(8,128)(2,1)S(1)}, bf16[176,2048]{1,0:T(8,128)(2,1)S(1)}, bf16[176,1024]{1,0:T(8,128)(2,1)S(1)}, bf16[176,1024]{1,0:T(8,128)(2,1)S(1)}) custom-call(bf16[512,704]{1,0:T(8,128)(2,1)S(1)} %get-tuple-element.106.refs_8_.refs_0_, ...), custom_call_target="tpu_custom_call" | custom-call | flops 2952790016 | bytes 8519680 | tf_op jit(solution)/shard_map/pallas_call | solution.py:395
  209.6 4.9 %collective-permute-done.42.refs_7_ = bf16[136,2048]{1,0:T(8,128)(2,1)S(1)} collective-permute-done((bf16[136,2048]{1,0:T(8,128)(2,1)S(1)}, bf16[136,2048]{1,0:T(8,128)(2,1)S(1)}, u32[]{:S(2)}, u32[]{:S(2)}) %collective-permute-start.42) | collective-permute-done | bytes 557088 | tf_op jit(solution)/shard_map/ppermute | solution.py:41
  217.5 9.4 %collective-permute-done.39.refs_4_ = bf16[136,2048]{1,0:T(8,128)(2,1)S(1)} collective-permute-done((bf16[136,2048]{1,0:T(8,128)(2,1)S(1)}, bf16[136,2048]{1,0:T(8,128)(2,1)S(1)}, u32[]{:S(2)}, u32[]{:S(2)}) %collective-permute-start.39) | collective-permute-done | bytes 557088 | tf_op jit(solution)/shard_map/ppermute | solution.py:41
  227.0 4.2 %collective-permute-start.40 = (bf16[136,2048]{1,0:T(8,128)(2,1)S(1)}, bf16[136,2048]{1,0:T(8,128)(2,1)S(1)}, u32[]{:S(2)}, u32[]{:S(2)}) collective-permute-start(bf16[136,2048]{1,0:T(8,128)(2,1)S(1)} %get-tuple-element.117), channel_id=1, source_target_pairs={{0,17},{1,16},{2,19},{3,18},{4,21},{5,20},{6,23},{7,22},{8,25},{9,... | collective-permute-start | bytes 1671176 | tf_op jit(solution)/shard_map/ppermute | solution.py:41
  231.1 4.6 %shard_map.123 = (bf16[128,2048]{1,0:T(8,128)(2,1)S(1)}, bf16[128,2048]{1,0:T(8,128)(2,1)S(1)}, bf16[128,2048]{1,0:T(8,128)(2,1)S(1)}, bf16[128,2048]{1,0:T(8,128)(2,1)S(1)}) custom-call(bf16[128,2048]{1,0:T(8,128)(2,1)S(1)} %get-tuple-element.81.refs_0_, bf16[128,2048]{1,0:T(8,128)(2,1)S(1)} %collective-permute-done.9.refs_1_, ...), custom_call_target="tpu_custom_call" | custom-call | flops 1073741824 | bytes 6324224 | tf_op jit(solution)/shard_map/pallas_call | solution.py:395
  235.8 6.6 %collective-permute-done.40.refs_5_ = bf16[136,2048]{1,0:T(8,128)(2,1)S(1)} collective-permute-done((bf16[136,2048]{1,0:T(8,128)(2,1)S(1)}, bf16[136,2048]{1,0:T(8,128)(2,1)S(1)}, u32[]{:S(2)}, u32[]{:S(2)}) %collective-permute-start.40) | collective-permute-done | bytes 557088 | tf_op jit(solution)/shard_map/ppermute | solution.py:41
  242.4 5.1 %collective-permute-done.50.from_ahead = bf16[176,2048]{1,0:T(8,128)(2,1)S(1)} collective-permute-done((bf16[176,2048]{1,0:T(8,128)(2,1)S(1)}, bf16[176,2048]{1,0:T(8,128)(2,1)S(1)}, u32[]{:S(2)}, u32[]{:S(2)}) %collective-permute-start.50) | collective-permute-done | bytes 720928 | tf_op jit(solution)/shard_map/ppermute | solution.py:506
  257.5 6.4 %collective-permute-done.21.refs_2_ = bf16[128,2048]{1,0:T(8,128)(2,1)S(1)} collective-permute-done((bf16[128,2048]{1,0:T(8,128)(2,1)S(1)}, bf16[128,2048]{1,0:T(8,128)(2,1)S(1)}, u32[]{:S(2)}, u32[]{:S(2)}) %collective-permute-start.21) | collective-permute-done | bytes 524320 | tf_op jit(solution)/shard_map/ppermute | solution.py:41
  263.8 3.7 %collective-permute-start.49 = (bf16[704,512]{1,0:T(8,128)(2,1)S(1)}, bf16[704,512]{1,0:T(8,128)(2,1)S(1)}, u32[]{:S(2)}, u32[]{:S(2)}) collective-permute-start(bf16[704,512]{1,0:T(8,128)(2,1)S(1)} %get-tuple-element.136), channel_id=1, source_target_pairs={{0,96},{32,0},{64,32},{96,64},{1,97},{33,1},{65,33},{97,65},{2,98}... | collective-permute-start | bytes 2162696 | tf_op jit(solution)/shard_map/ppermute | solution.py:506
  267.5 4.0 %shard_map.128 = (bf16[136,2048]{1,0:T(8,128)(2,1)S(1)}, bf16[136,2048]{1,0:T(8,128)(2,1)S(1)}, bf16[136,2048]{1,0:T(8,128)(2,1)S(1)}, bf16[136,2048]{1,0:T(8,128)(2,1)S(1)}) custom-call(bf16[136,2048]{1,0:T(8,128)(2,1)S(1)} %get-tuple-element.108.refs_0_, bf16[136,2048]{1,0:T(8,128)(2,1)S(1)} %collective-permute-done.32.refs_1_, ...), custom_call_target="tpu_custom_call" | custom-call | flops 536870912 | bytes 6717440 | tf_op jit(solution)/shard_map/pallas_call | solution.py:395
  278.6 10.2 %collective-permute-done.43.refs_1_ = bf16[136,2048]{1,0:T(8,128)(2,1)S(1)} collective-permute-done((bf16[136,2048]{1,0:T(8,128)(2,1)S(1)}, bf16[136,2048]{1,0:T(8,128)(2,1)S(1)}, u32[]{:S(2)}, u32[]{:S(2)}) %collective-permute-start.43) | collective-permute-done | bytes 557088 | tf_op jit(solution)/shard_map/ppermute | solution.py:41
  288.8 3.7 %collective-permute-done.44.refs_2_ = bf16[136,2048]{1,0:T(8,128)(2,1)S(1)} collective-permute-done((bf16[136,2048]{1,0:T(8,128)(2,1)S(1)}, bf16[136,2048]{1,0:T(8,128)(2,1)S(1)}, u32[]{:S(2)}, u32[]{:S(2)}) %collective-permute-start.44) | collective-permute-done | bytes 557088 | tf_op jit(solution)/shard_map/ppermute | solution.py:41
  292.5 10.7 %collective-permute-done.45.refs_3_ = bf16[136,2048]{1,0:T(8,128)(2,1)S(1)} collective-permute-done((bf16[136,2048]{1,0:T(8,128)(2,1)S(1)}, bf16[136,2048]{1,0:T(8,128)(2,1)S(1)}, u32[]{:S(2)}, u32[]{:S(2)}) %collective-permute-start.45) | collective-permute-done | bytes 557088 | tf_op jit(solution)/shard_map/ppermute | solution.py:41
  (107 shorter events, 88.7 us)
Async XLA Ops:
  0.6 40.3 %collective-permute-start = (bf16[128,2048]{1,0:T(8,128)(2,1)}, bf16[128,2048]{1,0:T(8,128)(2,1)S(1)}, u32[]{:S(2)}, u32[]{:S(2)}) collective-permute-start(bf16[128,2048]{1,0:T(8,128)(2,1)} %tokens.1), channel_id=1, source_target_pairs={{0,8},{1,9},{2,10},{3,11},{4,12},{5,13},{6,14},{7,15},{8,16},{9,17... | collective-permute-start | bytes 1572872 | tf_op jit(solution)/shard_map/ppermute | solution.py:41
  2.7 39.0 %collective-permute-start.2 = (bf16[128,2048]{1,0:T(8,128)(2,1)}, bf16[128,2048]{1,0:T(8,128)(2,1)S(1)}, u32[]{:S(2)}, u32[]{:S(2)}) collective-permute-start(bf16[128,2048]{1,0:T(8,128)(2,1)} %tokens.1), channel_id=1, source_target_pairs={{0,24},{1,25},{2,26},{3,27},{4,28},{5,29},{6,30},{7,31},{8,0},{9,1... | collective-permute-start | bytes 1572872 | tf_op jit(solution)/shard_map/ppermute | solution.py:41
  4.9 36.8 %collective-permute-start.1 = (bf16[128,2048]{1,0:T(8,128)(2,1)}, bf16[128,2048]{1,0:T(8,128)(2,1)S(1)}, u32[]{:S(2)}, u32[]{:S(2)}) collective-permute-start(bf16[128,2048]{1,0:T(8,128)(2,1)} %tokens.1), channel_id=1, source_target_pairs={{0,16},{1,17},{2,18},{3,19},{4,20},{5,21},{6,22},{7,23},{8,24},{9,... | collective-permute-start | bytes 1572872 | tf_op jit(solution)/shard_map/ppermute | solution.py:41
  6.7 64.3 %collective-permute-start.23 = (bf16[128,2048]{1,0:T(8,128)(2,1)}, bf16[128,2048]{1,0:T(8,128)(2,1)S(1)}, u32[]{:S(2)}, u32[]{:S(2)}) collective-permute-start(bf16[128,2048]{1,0:T(8,128)(2,1)} %cot.1), channel_id=1, source_target_pairs={{0,2},{1,3},{2,4},{3,5},{4,6},{5,7},{6,0},{7,1},{8,10},{9,11},{10,... | collective-permute-start | bytes 1572872 | tf_op jit(solution)/shard_map/ppermute | solution.py:41
  38.2 32.8 %collective-permute-start.25 = (bf16[128,2048]{1,0:T(8,128)(2,1)}, bf16[128,2048]{1,0:T(8,128)(2,1)S(1)}, u32[]{:S(2)}, u32[]{:S(2)}) collective-permute-start(bf16[128,2048]{1,0:T(8,128)(2,1)} %cot.1), channel_id=1, source_target_pairs={{0,6},{1,7},{2,0},{3,1},{4,2},{5,3},{6,4},{7,5},{8,14},{9,15},{10,... | collective-permute-start | bytes 1572872 | tf_op jit(solution)/shard_map/ppermute | solution.py:41
  41.0 33.5 %collective-permute-start.24 = (bf16[128,2048]{1,0:T(8,128)(2,1)}, bf16[128,2048]{1,0:T(8,128)(2,1)S(1)}, u32[]{:S(2)}, u32[]{:S(2)}) collective-permute-start(bf16[128,2048]{1,0:T(8,128)(2,1)} %cot.1), channel_id=1, source_target_pairs={{0,4},{1,5},{2,6},{3,7},{4,0},{5,1},{6,2},{7,3},{8,12},{9,13},{10,... | collective-permute-start | bytes 1572872 | tf_op jit(solution)/shard_map/ppermute | solution.py:41
  44.5 31.0 %collective-permute-start.6 = (bf16[128,2048]{1,0:T(8,128)(2,1)S(1)}, bf16[128,2048]{1,0:T(8,128)(2,1)S(1)}, u32[]{:S(2)}, u32[]{:S(2)}) collective-permute-start(bf16[128,2048]{1,0:T(8,128)(2,1)S(1)} %get-tuple-element.78), channel_id=1, source_target_pairs={{0,1},{1,0},{2,3},{3,2},{4,5},{5,4},{6,7},{7,6},{8,9},{9,8},{10,11... | collective-permute-start | bytes 1572872 | tf_op jit(solution)/shard_map/ppermute | solution.py:41
  71.0 23.0 %collective-permute-start.8 = (bf16[128,2048]{1,0:T(8,128)(2,1)S(1)}, bf16[128,2048]{1,0:T(8,128)(2,1)S(1)}, u32[]{:S(2)}, u32[]{:S(2)}) collective-permute-start(bf16[128,2048]{1,0:T(8,128)(2,1)S(1)} %get-tuple-element.80), channel_id=1, source_target_pairs={{0,3},{1,2},{2,5},{3,4},{4,7},{5,6},{6,1},{7,0},{8,11},{9,10},{10,... | collective-permute-start | bytes 1572872 | tf_op jit(solution)/shard_map/ppermute | solution.py:41
  71.0 37.9 %collective-permute-start.12 = (bf16[128,2048]{1,0:T(8,128)(2,1)S(1)}, bf16[128,2048]{1,0:T(8,128)(2,1)S(1)}, u32[]{:S(2)}, u32[]{:S(2)}) collective-permute-start(bf16[128,2048]{1,0:T(8,128)(2,1)S(1)} %get-tuple-element.85), channel_id=1, source_target_pairs={{0,4},{1,5},{2,6},{3,7},{4,0},{5,1},{6,2},{7,3},{8,12},{9,13},{10,... | collective-permute-start | bytes 1572872 | tf_op jit(solution)/shard_map/ppermute | solution.py:41
  74.5 36.9 %collective-permute-start.13 = (bf16[128,2048]{1,0:T(8,128)(2,1)S(1)}, bf16[128,2048]{1,0:T(8,128)(2,1)S(1)}, u32[]{:S(2)}, u32[]{:S(2)}) collective-permute-start(bf16[128,2048]{1,0:T(8,128)(2,1)S(1)} %get-tuple-element.86), channel_id=1, source_target_pairs={{0,5},{1,4},{2,7},{3,6},{4,1},{5,0},{6,3},{7,2},{8,13},{9,12},{10,... | collective-permute-start | bytes 1572872 | tf_op jit(solution)/shard_map/ppermute | solution.py:41
  75.5 39.9 %collective-permute-start.14 = (bf16[128,2048]{1,0:T(8,128)(2,1)S(1)}, bf16[128,2048]{1,0:T(8,128)(2,1)S(1)}, u32[]{:S(2)}, u32[]{:S(2)}) collective-permute-start(bf16[128,2048]{1,0:T(8,128)(2,1)S(1)} %get-tuple-element.87), channel_id=1, source_target_pairs={{0,6},{1,7},{2,0},{3,1},{4,2},{5,3},{6,4},{7,5},{8,14},{9,15},{10,... | collective-permute-start | bytes 1572872 | tf_op jit(solution)/shard_map/ppermute | solution.py:41
  86.4 33.4 %collective-permute-start.15 = (bf16[128,2048]{1,0:T(8,128)(2,1)S(1)}, bf16[128,2048]{1,0:T(8,128)(2,1)S(1)}, u32[]{:S(2)}, u32[]{:S(2)}) collective-permute-start(bf16[128,2048]{1,0:T(8,128)(2,1)S(1)} %get-tuple-element.88), channel_id=1, source_target_pairs={{0,7},{1,6},{2,1},{3,0},{4,3},{5,2},{6,5},{7,4},{8,15},{9,14},{10,... | collective-permute-start | bytes 1572872 | tf_op jit(solution)/shard_map/ppermute | solution.py:41
  94.0 26.3 %collective-permute-start.29 = (bf16[128,2048]{1,0:T(8,128)(2,1)S(1)}, bf16[128,2048]{1,0:T(8,128)(2,1)S(1)}, u32[]{:S(2)}, u32[]{:S(2)}) collective-permute-start(bf16[128,2048]{1,0:T(8,128)(2,1)S(1)} %get-tuple-element.98), channel_id=1, source_target_pairs={{0,16},{1,17},{2,18},{3,19},{4,20},{5,21},{6,22},{7,23},{8,24},{9,... | collective-permute-start | bytes 1572872 | tf_op jit(solution)/shard_map/ppermute | solution.py:41
  119.8 26.3 %collective-permute-start.34 = (bf16[128,2048]{1,0:T(8,128)(2,1)S(1)}, bf16[128,2048]{1,0:T(8,128)(2,1)S(1)}, u32[]{:S(2)}, u32[]{:S(2)}) collective-permute-start(bf16[128,2048]{1,0:T(8,128)(2,1)S(1)} %get-tuple-element.111), channel_id=1, source_target_pairs={{0,9},{1,8},{2,11},{3,10},{4,13},{5,12},{6,15},{7,14},{8,17},{9,16... | collective-permute-start | bytes 1572872 | tf_op jit(solution)/shard_map/ppermute | solution.py:41
  120.3 25.9 %collective-permute-start.35 = (bf16[128,2048]{1,0:T(8,128)(2,1)S(1)}, bf16[128,2048]{1,0:T(8,128)(2,1)S(1)}, u32[]{:S(2)}, u32[]{:S(2)}) collective-permute-start(bf16[128,2048]{1,0:T(8,128)(2,1)S(1)} %get-tuple-element.112), channel_id=1, source_target_pairs={{0,24},{1,25},{2,26},{3,27},{4,28},{5,29},{6,30},{7,31},{8,0},{9,1... | collective-permute-start | bytes 1572872 | tf_op jit(solution)/shard_map/ppermute | solution.py:41
  146.1 34.0 %collective-permute-start.19 = (bf16[128,2048]{1,0:T(8,128)(2,1)S(1)}, bf16[128,2048]{1,0:T(8,128)(2,1)S(1)}, u32[]{:S(2)}, u32[]{:S(2)}) collective-permute-start(bf16[128,2048]{1,0:T(8,128)(2,1)S(1)} %get-tuple-element.92), channel_id=1, source_target_pairs={{0,3},{1,2},{2,5},{3,4},{4,7},{5,6},{6,1},{7,0},{8,11},{9,10},{10,... | collective-permute-start | bytes 1572872 | tf_op jit(solution)/shard_map/ppermute | solution.py:41
  153.4 33.8 %collective-permute-start.9 = (bf16[128,2048]{1,0:T(8,128)(2,1)S(1)}, bf16[128,2048]{1,0:T(8,128)(2,1)S(1)}, u32[]{:S(2)}, u32[]{:S(2)}) collective-permute-start(bf16[128,2048]{1,0:T(8,128)(2,1)S(1)} %get-tuple-element.82), channel_id=1, source_target_pairs={{0,1},{1,0},{2,3},{3,2},{4,5},{5,4},{6,7},{7,6},{8,9},{9,8},{10,11... | collective-permute-start | bytes 1572872 | tf_op jit(solution)/shard_map/ppermute | solution.py:41
  153.8 34.3 %collective-permute-start.10 = (bf16[128,2048]{1,0:T(8,128)(2,1)S(1)}, bf16[128,2048]{1,0:T(8,128)(2,1)S(1)}, u32[]{:S(2)}, u32[]{:S(2)}) collective-permute-start(bf16[128,2048]{1,0:T(8,128)(2,1)S(1)} %get-tuple-element.83), channel_id=1, source_target_pairs={{0,6},{1,7},{2,0},{3,1},{4,2},{5,3},{6,4},{7,5},{8,14},{9,15},{10,... | collective-permute-start | bytes 1572872 | tf_op jit(solution)/shard_map/ppermute | solution.py:41
  156.9 32.6 %collective-permute-start.11 = (bf16[128,2048]{1,0:T(8,128)(2,1)S(1)}, bf16[128,2048]{1,0:T(8,128)(2,1)S(1)}, u32[]{:S(2)}, u32[]{:S(2)}) collective-permute-start(bf16[128,2048]{1,0:T(8,128)(2,1)S(1)} %get-tuple-element.84), channel_id=1, source_target_pairs={{0,7},{1,6},{2,1},{3,0},{4,3},{5,2},{6,5},{7,4},{8,15},{9,14},{10,... | collective-permute-start | bytes 1572872 | tf_op jit(solution)/shard_map/ppermute | solution.py:41
  169.0 28.8 %collective-permute-start.37 = (bf16[136,2048]{1,0:T(8,128)(2,1)S(1)}, bf16[136,2048]{1,0:T(8,128)(2,1)S(1)}, u32[]{:S(2)}, u32[]{:S(2)}) collective-permute-start(bf16[136,2048]{1,0:T(8,128)(2,1)S(1)} %get-tuple-element.114), channel_id=1, source_target_pairs={{0,24},{1,25},{2,26},{3,27},{4,28},{5,29},{6,30},{7,31},{8,0},{9,1... | collective-permute-start | bytes 1671176 | tf_op jit(solution)/shard_map/ppermute | solution.py:41
  188.1 26.4 %collective-permute-start.42 = (bf16[136,2048]{1,0:T(8,128)(2,1)S(1)}, bf16[136,2048]{1,0:T(8,128)(2,1)S(1)}, u32[]{:S(2)}, u32[]{:S(2)}) collective-permute-start(bf16[136,2048]{1,0:T(8,128)(2,1)S(1)} %get-tuple-element.119), channel_id=1, source_target_pairs={{0,9},{1,8},{2,11},{3,10},{4,13},{5,12},{6,15},{7,14},{8,17},{9,16... | collective-permute-start | bytes 1671176 | tf_op jit(solution)/shard_map/ppermute | solution.py:41
  189.5 28.1 %collective-permute-start.32 = (bf16[136,2048]{1,0:T(8,128)(2,1)S(1)}, bf16[136,2048]{1,0:T(8,128)(2,1)S(1)}, u32[]{:S(2)}, u32[]{:S(2)}) collective-permute-start(bf16[136,2048]{1,0:T(8,128)(2,1)S(1)} %get-tuple-element.109), channel_id=1, source_target_pairs={{0,1},{1,0},{2,3},{3,2},{4,5},{5,4},{6,7},{7,6},{8,9},{9,8},{10,11... | collective-permute-start | bytes 1671176 | tf_op jit(solution)/shard_map/ppermute | solution.py:41
  197.8 53.9 %collective-permute-start.46 = (bf16[1408,512]{1,0:T(8,128)(2,1)S(1)}, bf16[1408,512]{1,0:T(8,128)(2,1)S(1)}, u32[]{:S(2)}, u32[]{:S(2)}) collective-permute-start(bf16[1408,512]{1,0:T(8,128)(2,1)S(1)} %get-tuple-element.131), channel_id=1, source_target_pairs={{0,96},{32,0},{64,32},{96,64},{1,97},{33,1},{65,33},{97,65},{2,98}... | collective-permute-start | bytes 4325384 | tf_op jit(solution)/shard_map/ppermute | solution.py:506
  200.9 50.9 %collective-permute-start.47 = (bf16[1408,512]{1,0:T(8,128)(2,1)S(1)}, bf16[1408,512]{1,0:T(8,128)(2,1)S(1)}, u32[]{:S(2)}, u32[]{:S(2)}) collective-permute-start(bf16[1408,512]{1,0:T(8,128)(2,1)S(1)} %get-tuple-element.132), channel_id=1, source_target_pairs={{0,32},{32,64},{64,96},{96,0},{1,33},{33,65},{65,97},{97,1},{2,34}... | collective-permute-start | bytes 4325384 | tf_op jit(solution)/shard_map/ppermute | solution.py:506
  203.9 23.0 %collective-permute-start.39 = (bf16[136,2048]{1,0:T(8,128)(2,1)S(1)}, bf16[136,2048]{1,0:T(8,128)(2,1)S(1)}, u32[]{:S(2)}, u32[]{:S(2)}) collective-permute-start(bf16[136,2048]{1,0:T(8,128)(2,1)S(1)} %get-tuple-element.116), channel_id=1, source_target_pairs={{0,16},{1,17},{2,18},{3,19},{4,20},{5,21},{6,22},{7,23},{8,24},{9,... | collective-permute-start | bytes 1671176 | tf_op jit(solution)/shard_map/ppermute | solution.py:41
  214.5 33.0 %collective-permute-start.50 = (bf16[176,2048]{1,0:T(8,128)(2,1)S(1)}, bf16[176,2048]{1,0:T(8,128)(2,1)S(1)}, u32[]{:S(2)}, u32[]{:S(2)}) collective-permute-start(bf16[176,2048]{1,0:T(8,128)(2,1)S(1)} %get-tuple-element.138), channel_id=1, source_target_pairs={{0,96},{32,0},{64,32},{96,64},{1,97},{33,1},{65,33},{97,65},{2,98}... | collective-permute-start | bytes 2162696 | tf_op jit(solution)/shard_map/ppermute | solution.py:506
  217.5 33.4 %collective-permute-start.51 = (bf16[176,2048]{1,0:T(8,128)(2,1)S(1)}, bf16[176,2048]{1,0:T(8,128)(2,1)S(1)}, u32[]{:S(2)}, u32[]{:S(2)}) collective-permute-start(bf16[176,2048]{1,0:T(8,128)(2,1)S(1)} %get-tuple-element.139), channel_id=1, source_target_pairs={{0,32},{32,64},{64,96},{96,0},{1,33},{33,65},{65,97},{97,1},{2,34}... | collective-permute-start | bytes 2162696 | tf_op jit(solution)/shard_map/ppermute | solution.py:506
  251.7 23.8 %collective-permute-start.52 = (bf16[176,1024]{1,0:T(8,128)(2,1)S(1)}, bf16[176,1024]{1,0:T(8,128)(2,1)S(1)}, u32[]{:S(2)}, u32[]{:S(2)}) collective-permute-start(bf16[176,1024]{1,0:T(8,128)(2,1)S(1)} %get-tuple-element.142), channel_id=1, source_target_pairs={{0,32},{32,64},{64,96},{96,0},{1,33},{33,65},{65,97},{97,1},{2,34}... | collective-permute-start | bytes 1081352 | tf_op jit(solution)/shard_map/ppermute | solution.py:506
  251.8 24.4 %collective-permute-start.53 = (bf16[176,1024]{1,0:T(8,128)(2,1)S(1)}, bf16[176,1024]{1,0:T(8,128)(2,1)S(1)}, u32[]{:S(2)}, u32[]{:S(2)}) collective-permute-start(bf16[176,1024]{1,0:T(8,128)(2,1)S(1)} %get-tuple-element.143), channel_id=1, source_target_pairs={{0,96},{32,0},{64,32},{96,64},{1,97},{33,1},{65,33},{97,65},{2,98}... | collective-permute-start | bytes 1081352 | tf_op jit(solution)/shard_map/ppermute | solution.py:506
  256.4 47.8 %collective-permute-start.48 = (bf16[704,512]{1,0:T(8,128)(2,1)S(1)}, bf16[704,512]{1,0:T(8,128)(2,1)S(1)}, u32[]{:S(2)}, u32[]{:S(2)}) collective-permute-start(bf16[704,512]{1,0:T(8,128)(2,1)S(1)} %get-tuple-element.135), channel_id=1, source_target_pairs={{0,32},{32,64},{64,96},{96,0},{1,33},{33,65},{65,97},{97,1},{2,34}... | collective-permute-start | bytes 2162696 | tf_op jit(solution)/shard_map/ppermute | solution.py:506
  263.8 40.4 %collective-permute-start.49 = (bf16[704,512]{1,0:T(8,128)(2,1)S(1)}, bf16[704,512]{1,0:T(8,128)(2,1)S(1)}, u32[]{:S(2)}, u32[]{:S(2)}) collective-permute-start(bf16[704,512]{1,0:T(8,128)(2,1)S(1)} %get-tuple-element.136), channel_id=1, source_target_pairs={{0,96},{32,0},{64,32},{96,64},{1,97},{33,1},{65,33},{97,65},{2,98}... | collective-permute-start | bytes 2162696 | tf_op jit(solution)/shard_map/ppermute | solution.py:506
  276.2 27.0 %collective-permute-start.45 = (bf16[136,2048]{1,0:T(8,128)(2,1)S(1)}, bf16[136,2048]{1,0:T(8,128)(2,1)S(1)}, u32[]{:S(2)}, u32[]{:S(2)}) collective-permute-start(bf16[136,2048]{1,0:T(8,128)(2,1)S(1)} %get-tuple-element.123), channel_id=1, source_target_pairs={{0,2},{1,3},{2,4},{3,5},{4,6},{5,7},{6,0},{7,1},{8,10},{9,11},{10,... | collective-permute-start | bytes 1671176 | tf_op jit(solution)/shard_map/ppermute | solution.py:41
  (28 other events, 442.3 us)
where the time goes:
time: 309 us; the launch traced here: 306 us
  waiting for transfers between devices  163 us (53%)
  starting transfers between devices  76.3 us (25%)
  Pallas kernels  57.8 us (19%)
  local copies, waits for them, and re-layouts  4.23 us (1%)
  other arithmetic  3.75 us (1%)
    ppermute x46, waiting for transfers between devices, move(): return lax.ppermute(value, 'ep', shift_pairs(axis, step, flip))  157 us
    ppermute x46, starting transfers between devices, move(): return lax.ppermute(value, 'ep', shift_pairs(axis, step, flip))  62.1 us
    pallas_call x16, Pallas kernels, call(): pl.pallas_call(body, out_shape=tuple(outs), in_specs=[vmem] * len(args),...  57.8 us
    ppermute x8, starting transfers between devices, pass_on(): return lax.ppermute(value, 'rep', [(r, (r + step) % 4) for r in range(4)])  14.1 us
    ppermute x8, waiting for transfers between devices, pass_on(): return lax.ppermute(value, 'rep', [(r, (r + step) % 4) for r in range(4)])  6.45 us
  transfers between devices with their start and end apart: 54, of which 28 were waited for; matrix products, arithmetic and copies ran while one was open for 1% of the time, Pallas kernels for 19%

commit v1 on v0

--- a/solution.py
+++ b/solution.py
@@ -320,7 +320,7 @@
 
 def column_grad_body(order, arrays, *refs):
     gates, ups, blocks = refs[:arrays], refs[arrays : 2 * arrays], refs[2 * arrays : 2 * arrays + 8]
-    own, ahead, behind, ahead_kept, behind_kept, turned, piece = refs[2 * arrays + 8 :]
+    own, ahead, behind, ahead_kept, behind_kept, turned, piece, columns = refs[2 * arrays + 8 :]
     rep = lax.axis_index("rep")
     width = own.shape[1]
     hidden = gates[0].shape[1]
@@ -331,9 +331,13 @@
 
     def chunk(k, carry):
         start = pl.multiple_of(((rep + k) & 3) * width, LANES)
-        right = in_cot_order(blocks, pl.ds(start, width), order)
-        for half in range(2):
-            piece[half] = jnp.dot(turned[half], right, preferred_element_type=F32).astype(BF16)
+        columns[...] = in_cot_order(blocks, pl.ds(start, width), order)
+
+        def product(half, inner):
+            piece[half] = jnp.dot(turned[half], columns[...], preferred_element_type=F32).astype(BF16)
+            return inner
+
+        lax.fori_loop(0, 2, product, 0)
         for n in range(4):
 
             @pl.when(k == n)
@@ -448,7 +452,7 @@
     cots = [move(sent_cot[q], "z", q >> 1, q & 1) for q in range(DESTS)]
 
     unit = 2 * ROWS * width * hidden
-    groups = ((0, 1), (2, 3))
+    groups = ((0,), (1, 3), (2,))
     place = hidden_slices(groups)
     out_blocks, gates, ups, acts = {}, [], [], []
     for ks in groups:
@@ -499,7 +503,8 @@
     both_parts = call(
         functools.partial(column_grad_body, order, len(back_groups)),
         gate_grads + up_grads + rows, chunks(2 * hidden, width // 4, 0), 16 * unit,
-        [pltpu.VMEM((2, hidden, DESTS * ROWS), BF16), pltpu.VMEM((2, hidden, width // 4), BF16)],
+        [pltpu.VMEM((2, hidden, DESTS * ROWS), BF16), pltpu.VMEM((2, hidden, width // 4), BF16),
+         pltpu.VMEM((DESTS * ROWS, width // 4), BF16)],
     )
 
     def pass_on(value, step):

time: 309 us -> 292 us (0.945)
  starting transfers between devices: 76.3 us -> 66.2 us
  waiting for transfers between devices: 163 us -> 155 us
    ppermute x46, waiting for transfers between devices: 157 us -> 146 us  [move(): return lax.ppermute(value, 'ep', shift_pairs(axis, step, flip))]
    ppermute x46, starting transfers between devices: 62.1 us -> 52.3 us  [move(): return lax.ppermute(value, 'ep', shift_pairs(axis, step, flip))]
    ppermute x8, waiting for transfers between devices: 6.45 us -> 9.68 us  [pass_on(): return lax.ppermute(value, 'rep', [(r, (r + step) % 4) for r in range(4)])]
    pallas_call x16 -> x17, Pallas kernels: 57.8 us -> 59.4 us  [call(): pl.pallas_call(body, out_shape=tuple(outs), in_specs=[vmem] * len(args),...]
  transfers between devices with their start and end apart: 54 -> 54, of which waited for: 28 -> 29; matrix products, arithmetic and copies ran while one was open for 1% -> 1% of each run, Pallas kernels for 19% -> 20%
where the time goes in v1:
time: 292 us; the launch traced here: 291 us
  waiting for transfers between devices  155 us (53%)
  starting transfers between devices  66.2 us (23%)
  Pallas kernels  59.4 us (20%)
  local copies, waits for them, and re-layouts  5.71 us (2%)
  other arithmetic  3.74 us (1%)
    ppermute x46, waiting for transfers between devices, move(): return lax.ppermute(value, 'ep', shift_pairs(axis, step, flip))  146 us
    pallas_call x17, Pallas kernels, call(): pl.pallas_call(body, out_shape=tuple(outs), in_specs=[vmem] * len(args),...  59.4 us
    ppermute x46, starting transfers between devices, move(): return lax.ppermute(value, 'ep', shift_pairs(axis, step, flip))  52.3 us
    ppermute x8, starting transfers between devices, pass_on(): return lax.ppermute(value, 'rep', [(r, (r + step) % 4) for r in range(4)])  13.9 us
    ppermute x8, waiting for transfers between devices, pass_on(): return lax.ppermute(value, 'rep', [(r, (r + step) % 4) for r in range(4)])  9.68 us
  transfers between devices with their start and end apart: 54, of which 29 were waited for; matrix products, arithmetic and copies ran while one was open for 1% of the time, Pallas kernels for 20%

profile of v1, /device:TPU:0, one launch (start us, length us, event | category | flops | bytes accessed | tf_op | source)
XLA Modules:
  0.0 291.2 jit_solution(11832363854028654332)
XLA Ops:
  13.4 14.6 %collective-permute-done.5.refs_7_.refs_11_ = f32[16,128]{1,0:T(8,128)S(1)} collective-permute-done((f32[16,128]{1,0:T(8,128)S(1)}, f32[16,128]{1,0:T(8,128)S(1)}, u32[]{:S(2)}, u32[]{:S(2)}) %collective-permute-start.5) | collective-permute-done | bytes 8224 | tf_op jit(solution)/shard_map/ppermute | solution.py:41
  40.9 15.6 %collective-permute-done.28.refs_7_.refs_11_ = f32[16,128]{1,0:T(8,128)S(1)} collective-permute-done((f32[16,128]{1,0:T(8,128)S(1)}, f32[16,128]{1,0:T(8,128)S(1)}, u32[]{:S(2)}, u32[]{:S(2)}) %collective-permute-start.28) | collective-permute-done | bytes 8224 | tf_op jit(solution)/shard_map/ppermute | solution.py:41
  62.6 4.4 %collective-permute-done.26.refs_5_.refs_9_ = f32[16,128]{1,0:T(8,128)S(1)} collective-permute-done((f32[16,128]{1,0:T(8,128)S(1)}, f32[16,128]{1,0:T(8,128)S(1)}, u32[]{:S(2)}, u32[]{:S(2)}) %collective-permute-start.26) | collective-permute-done | bytes 8224 | tf_op jit(solution)/shard_map/ppermute | solution.py:41
  67.0 3.3 %collective-permute-start.10 = (bf16[128,2048]{1,0:T(8,128)(2,1)S(1)}, bf16[128,2048]{1,0:T(8,128)(2,1)S(1)}, u32[]{:S(2)}, u32[]{:S(2)}) collective-permute-start(bf16[128,2048]{1,0:T(8,128)(2,1)S(1)} %get-tuple-element.86), channel_id=1, source_target_pairs={{0,6},{1,7},{2,0},{3,1},{4,2},{5,3},{6,4},{7,5},{8,14},{9,15},{10,... | collective-permute-start | bytes 1572872 | tf_op jit(solution)/shard_map/ppermute | solution.py:41
  72.9 3.2 %shard_map.126 = (bf16[128,2048]{1,0:T(8,128)(2,1)S(1)}, bf16[128,2048]{1,0:T(8,128)(2,1)S(1)}, bf16[128,2048]{1,0:T(8,128)(2,1)S(1)}, bf16[128,2048]{1,0:T(8,12...) custom-call(bf16[128,2048]{1,0:T(8,128)(2,1)S(1)} %get-tuple-element, ...), custom_call_target="tpu_custom_call" | custom-call | flops 536870912 | bytes 6324224 | tf_op jit(solution)/shard_map/pallas_call | solution.py:399
  76.2 6.3 %collective-permute-done.8.refs_0_.refs_6_ = bf16[128,2048]{1,0:T(8,128)(2,1)S(1)} collective-permute-done((bf16[128,2048]{1,0:T(8,128)(2,1)S(1)}, bf16[128,2048]{1,0:T(8,128)(2,1)S(1)}, u32[]{:S(2)}, u32[]{:S(2)}) %collective-permute-start.8) | collective-permute-done | bytes 524320 | tf_op jit(solution)/shard_map/ppermute | solution.py:41
  82.4 7.6 %collective-permute-done.9.refs_1_.refs_7_ = bf16[128,2048]{1,0:T(8,128)(2,1)S(1)} collective-permute-done((bf16[128,2048]{1,0:T(8,128)(2,1)S(1)}, bf16[128,2048]{1,0:T(8,128)(2,1)S(1)}, u32[]{:S(2)}, u32[]{:S(2)}) %collective-permute-start.9) | collective-permute-done | bytes 524320 | tf_op jit(solution)/shard_map/ppermute | solution.py:41
  91.9 12.8 %collective-permute-done.10.refs_2_.refs_10_ = bf16[128,2048]{1,0:T(8,128)(2,1)S(1)} collective-permute-done((bf16[128,2048]{1,0:T(8,128)(2,1)S(1)}, bf16[128,2048]{1,0:T(8,128)(2,1)S(1)}, u32[]{:S(2)}, u32[]{:S(2)}) %collective-permute-start.10) | collective-permute-done | bytes 524320 | tf_op jit(solution)/shard_map/ppermute | solution.py:41
  111.0 4.0 %shard_map.123 = (bf16[128,2048]{1,0:T(8,128)(2,1)S(1)}, bf16[128,2048]{1,0:T(8,128)(2,1)S(1)}, bf16[256,704]{1,0:T(8,128)(2,1)S(1)}, bf16[256,704]{1,0:T(8,128)(2,1)S(1)}, bf16[256,704]{1,0:T(8,128)(2,1)S(1)}) custom-call(bf16[128,2048]{1,0:T(8,128)(2,1)S(1)} %collective-permute-done.14.refs_0_.refs_8_, ...), custom_call_target="tpu_custom_call" | custom-call | flops 2214592512 | bytes 11829248 | tf_op jit(solution)/shard_map/pallas_call | solution.py:399
  115.6 4.4 %collective-permute-start.34 = (bf16[128,2048]{1,0:T(8,128)(2,1)S(1)}, bf16[128,2048]{1,0:T(8,128)(2,1)S(1)}, u32[]{:S(2)}, u32[]{:S(2)}) collective-permute-start(bf16[128,2048]{1,0:T(8,128)(2,1)S(1)} %get-tuple-element.117), channel_id=1, source_target_pairs={{0,9},{1,8},{2,11},{3,10},{4,13},{5,12},{6,15},{7,14},{8,17},{9,16... | collective-permute-start | bytes 1572872 | tf_op jit(solution)/shard_map/ppermute | solution.py:41
  123.3 7.3 %collective-permute-done.33.refs_0_.refs_5_ = bf16[128,2048]{1,0:T(8,128)(2,1)S(1)} collective-permute-done((bf16[128,2048]{1,0:T(8,128)(2,1)S(1)}, bf16[128,2048]{1,0:T(8,128)(2,1)S(1)}, u32[]{:S(2)}, u32[]{:S(2)}) %collective-permute-start.33) | collective-permute-done | bytes 524320 | tf_op jit(solution)/shard_map/ppermute | solution.py:41
  130.6 3.9 %shard_map.121 = (bf16[128,2048]{1,0:T(8,128)(2,1)S(1)}, bf16[128,2048]{1,0:T(8,128)(2,1)S(1)}, bf16[256,704]{1,0:T(8,128)(2,1)S(1)}, bf16[256,704]{1,0:T(8,128)(2,1)S(1)}, bf16[256,704]{1,0:T(8,128)(2,1)S(1)}) custom-call(bf16[128,2048]{1,0:T(8,128)(2,1)S(1)} %get-tuple-element.80.refs_0_.refs_4_, ...), custom_call_target="tpu_custom_call" | custom-call | flops 2214592512 | bytes 11829248 | tf_op jit(solution)/shard_map/pallas_call | solution.py:399
  134.5 7.2 %shard_map.122 = (bf16[128,2048]{1,0:T(8,128)(2,1)S(1)}, bf16[128,2048]{1,0:T(8,128)(2,1)S(1)}, bf16[128,2048]{1,0:T(8,128)(2,1)S(1)}, bf16[128,2048]{1,0:T(8,12...) custom-call(bf16[128,2048]{1,0:T(8,128)(2,1)S(1)} %collective-permute-done.8.r, ...), custom_call_target="tpu_custom_call" | custom-call | flops 4429185024 | bytes 15007744 | tf_op jit(solution)/shard_map/pallas_call | solution.py:399
  142.3 3.7 %collective-permute-start.12 = (bf16[128,2048]{1,0:T(8,128)(2,1)S(1)}, bf16[128,2048]{1,0:T(8,128)(2,1)S(1)}, u32[]{:S(2)}, u32[]{:S(2)}) collective-permute-start(bf16[128,2048]{1,0:T(8,128)(2,1)S(1)} %get-tuple-element.88), channel_id=1, source_target_pairs={{0,6},{1,7},{2,0},{3,1},{4,2},{5,3},{6,4},{7,5},{8,14},{9,15},{10,... | collective-permute-start | bytes 1572872 | tf_op jit(solution)/shard_map/ppermute | solution.py:41
  149.6 6.1 %shard_map.128 = (bf16[136,2048]{1,0:T(8,128)(2,1)S(1)}, bf16[136,2048]{1,0:T(8,128)(2,1)S(1)}, bf16[136,2048]{1,0:T(8,128)(2,1)S(1)}, bf16[136,2048]{1,0:T(8,12...) custom-call(bf16[128,2048]{1,0:T(8,128)(2,1)S(1)} %collective-permute-done.33.refs_0_.refs_5_, ...), custom_call_target="tpu_custom_call" | custom-call | flops 4429185024 | bytes 18743296 | tf_op jit(solution)/shard_map/pallas_call | solution.py:399
  160.1 6.2 %shard_map.127 = (bf16[136,2048]{1,0:T(8,128)(2,1)S(1)}, bf16[136,2048]{1,0:T(8,128)(2,1)S(1)}, bf16[136,2048]{1,0:T(8,128)(2,1)S(1)}, bf16[136,2048]{1,0:T(8,12...) custom-call(bf16[128,2048]{1,0:T(8,128)(2,1)S(1)} %collective-permute-done.29.refs_0_.refs_7_, ...), custom_call_target="tpu_custom_call" | custom-call | flops 4429185024 | bytes 18743296 | tf_op jit(solution)/shard_map/pallas_call | solution.py:399
  166.2 3.7 %collective-permute-done.13.refs_3_ = bf16[128,2048]{1,0:T(8,128)(2,1)S(1)} collective-permute-done((bf16[128,2048]{1,0:T(8,128)(2,1)S(1)}, bf16[128,2048]{1,0:T(8,128)(2,1)S(1)}, u32[]{:S(2)}, u32[]{:S(2)}) %collective-permute-start.13) | collective-permute-done | bytes 524320 | tf_op jit(solution)/shard_map/ppermute | solution.py:41
  172.7 8.9 %shard_map.131 = (bf16[1408,512]{1,0:T(8,128)(2,1)S(1)}, bf16[1408,512]{1,0:T(8,128)(2,1)S(1)}, bf16[1408,512]{1,0:T(8,128)(2,1)S(1)}, bf16[704,512]{1,0:T(8,128)(2,1)S(1)}, bf16[704,512]{1,0:T(8,128)(2,1)S(1)}) custom-call(bf16[512,704]{1,0:T(8,128)(2,1)S(1)} %get-tuple-element.132.refs_0_, bf16[512,704]{1,0:T(8,128)(2,1)S(1)} %get-tuple-element.133.refs_1_, ...), custom_call_target="tpu_custom_call" | custom-call | flops 5905580032 | bytes 12845056 | tf_op jit(solution)/shard_map/pallas_call | solution.py:399
  181.7 3.1 %collective-permute-start.46 = (bf16[1408,512]{1,0:T(8,128)(2,1)S(1)}, bf16[1408,512]{1,0:T(8,128)(2,1)S(1)}, u32[]{:S(2)}, u32[]{:S(2)}) collective-permute-start(bf16[1408,512]{1,0:T(8,128)(2,1)S(1)} %get-tuple-element.137), channel_id=1, source_target_pairs={{0,96},{32,0},{64,32},{96,64},{1,97},{33,1},{65,33},{97,65},{2,98}... | collective-permute-start | bytes 4325384 | tf_op jit(solution)/shard_map/ppermute | solution.py:511
  187.0 4.3 %shard_map.133 = (bf16[176,2048]{1,0:T(8,128)(2,1)S(1)}, bf16[176,2048]{1,0:T(8,128)(2,1)S(1)}, bf16[176,2048]{1,0:T(8,128)(2,1)S(1)}, bf16[176,1024]{1,0:T(8,128)(2,1)S(1)}, bf16[176,1024]{1,0:T(8,128)(2,1)S(1)}) custom-call(bf16[256,704]{1,0:T(8,128)(2,1)S(1)} %get-tuple-element.111.refs_10_.refs_0_, ...), custom_call_target="tpu_custom_call" | custom-call | flops 2952790016 | bytes 8519680 | tf_op jit(solution)/shard_map/pallas_call | solution.py:399
  191.3 7.0 %collective-permute-done.42.refs_7_ = bf16[136,2048]{1,0:T(8,128)(2,1)S(1)} collective-permute-done((bf16[136,2048]{1,0:T(8,128)(2,1)S(1)}, bf16[136,2048]{1,0:T(8,128)(2,1)S(1)}, u32[]{:S(2)}, u32[]{:S(2)}) %collective-permute-start.42) | collective-permute-done | bytes 557088 | tf_op jit(solution)/shard_map/ppermute | solution.py:41
  201.4 8.6 %collective-permute-done.39.refs_4_ = bf16[136,2048]{1,0:T(8,128)(2,1)S(1)} collective-permute-done((bf16[136,2048]{1,0:T(8,128)(2,1)S(1)}, bf16[136,2048]{1,0:T(8,128)(2,1)S(1)}, u32[]{:S(2)}, u32[]{:S(2)}) %collective-permute-start.39) | collective-permute-done | bytes 557088 | tf_op jit(solution)/shard_map/ppermute | solution.py:41
  210.9 4.6 %shard_map.124 = (bf16[128,2048]{1,0:T(8,128)(2,1)S(1)}, bf16[128,2048]{1,0:T(8,128)(2,1)S(1)}, bf16[128,2048]{1,0:T(8,128)(2,1)S(1)}, bf16[128,2048]{1,0:T(8,128)(2,1)S(1)}) custom-call(bf16[128,2048]{1,0:T(8,128)(2,1)S(1)} %get-tuple-element.82.refs_0_, bf16[128,2048]{1,0:T(8,128)(2,1)S(1)} %collective-permute-done.7.refs_1_, ...), custom_call_target="tpu_custom_call" | custom-call | flops 1073741824 | bytes 6324224 | tf_op jit(solution)/shard_map/pallas_call | solution.py:399
  215.5 7.5 %collective-permute-done.40.refs_5_ = bf16[136,2048]{1,0:T(8,128)(2,1)S(1)} collective-permute-done((bf16[136,2048]{1,0:T(8,128)(2,1)S(1)}, bf16[136,2048]{1,0:T(8,128)(2,1)S(1)}, u32[]{:S(2)}, u32[]{:S(2)}) %collective-permute-start.40) | collective-permute-done | bytes 557088 | tf_op jit(solution)/shard_map/ppermute | solution.py:41
  223.3 8.3 %collective-permute-done.50.from_ahead = bf16[176,2048]{1,0:T(8,128)(2,1)S(1)} collective-permute-done((bf16[176,2048]{1,0:T(8,128)(2,1)S(1)}, bf16[176,2048]{1,0:T(8,128)(2,1)S(1)}, u32[]{:S(2)}, u32[]{:S(2)}) %collective-permute-start.50) | collective-permute-done | bytes 720928 | tf_op jit(solution)/shard_map/ppermute | solution.py:511
  236.0 3.2 %collective-permute-start.53 = (bf16[176,1024]{1,0:T(8,128)(2,1)S(1)}, bf16[176,1024]{1,0:T(8,128)(2,1)S(1)}, u32[]{:S(2)}, u32[]{:S(2)}) collective-permute-start(bf16[176,1024]{1,0:T(8,128)(2,1)S(1)} %get-tuple-element.149), channel_id=1, source_target_pairs={{0,96},{32,0},{64,32},{96,64},{1,97},{33,1},{65,33},{97,65},{2,98}... | collective-permute-start | bytes 1081352 | tf_op jit(solution)/shard_map/ppermute | solution.py:511
  240.4 7.5 %collective-permute-done.21.refs_2_ = bf16[128,2048]{1,0:T(8,128)(2,1)S(1)} collective-permute-done((bf16[128,2048]{1,0:T(8,128)(2,1)S(1)}, bf16[128,2048]{1,0:T(8,128)(2,1)S(1)}, u32[]{:S(2)}, u32[]{:S(2)}) %collective-permute-start.21) | collective-permute-done | bytes 524320 | tf_op jit(solution)/shard_map/ppermute | solution.py:41
  247.9 3.7 %collective-permute-start.49 = (bf16[704,512]{1,0:T(8,128)(2,1)S(1)}, bf16[704,512]{1,0:T(8,128)(2,1)S(1)}, u32[]{:S(2)}, u32[]{:S(2)}) collective-permute-start(bf16[704,512]{1,0:T(8,128)(2,1)S(1)} %get-tuple-element.142), channel_id=1, source_target_pairs={{0,96},{32,0},{64,32},{96,64},{1,97},{33,1},{65,33},{97,65},{2,98}... | collective-permute-start | bytes 2162696 | tf_op jit(solution)/shard_map/ppermute | solution.py:511
  251.6 4.0 %shard_map.129 = (bf16[136,2048]{1,0:T(8,128)(2,1)S(1)}, bf16[136,2048]{1,0:T(8,128)(2,1)S(1)}, bf16[136,2048]{1,0:T(8,128)(2,1)S(1)}, bf16[136,2048]{1,0:T(8,128)(2,1)S(1)}) custom-call(bf16[136,2048]{1,0:T(8,128)(2,1)S(1)} %get-tuple-element.114.refs_0_, bf16[136,2048]{1,0:T(8,128)(2,1)S(1)} %collective-permute-done.32.refs_1_, ...), custom_call_target="tpu_custom_call" | custom-call | flops 536870912 | bytes 6717440 | tf_op jit(solution)/shard_map/pallas_call | solution.py:399
  262.9 10.2 %collective-permute-done.43.refs_1_ = bf16[136,2048]{1,0:T(8,128)(2,1)S(1)} collective-permute-done((bf16[136,2048]{1,0:T(8,128)(2,1)S(1)}, bf16[136,2048]{1,0:T(8,128)(2,1)S(1)}, u32[]{:S(2)}, u32[]{:S(2)}) %collective-permute-start.43) | collective-permute-done | bytes 557088 | tf_op jit(solution)/shard_map/ppermute | solution.py:41
  273.1 4.3 %collective-permute-done.44.refs_2_ = bf16[136,2048]{1,0:T(8,128)(2,1)S(1)} collective-permute-done((bf16[136,2048]{1,0:T(8,128)(2,1)S(1)}, bf16[136,2048]{1,0:T(8,128)(2,1)S(1)}, u32[]{:S(2)}, u32[]{:S(2)}) %collective-permute-start.44) | collective-permute-done | bytes 557088 | tf_op jit(solution)/shard_map/ppermute | solution.py:41
  277.3 10.7 %collective-permute-done.45.refs_3_ = bf16[136,2048]{1,0:T(8,128)(2,1)S(1)} collective-permute-done((bf16[136,2048]{1,0:T(8,128)(2,1)S(1)}, bf16[136,2048]{1,0:T(8,128)(2,1)S(1)}, u32[]{:S(2)}, u32[]{:S(2)}) %collective-permute-start.45) | collective-permute-done | bytes 557088 | tf_op jit(solution)/shard_map/ppermute | solution.py:41
  (108 shorter events, 80.2 us)
Async XLA Ops:
  0.6 35.4 %collective-permute-start = (bf16[128,2048]{1,0:T(8,128)(2,1)}, bf16[128,2048]{1,0:T(8,128)(2,1)S(1)}, u32[]{:S(2)}, u32[]{:S(2)}) collective-permute-start(bf16[128,2048]{1,0:T(8,128)(2,1)} %tokens.1), channel_id=1, source_target_pairs={{0,8},{1,9},{2,10},{3,11},{4,12},{5,13},{6,14},{7,15},{8,16},{9,17... | collective-permute-start | bytes 1572872 | tf_op jit(solution)/shard_map/ppermute | solution.py:41
  2.7 34.1 %collective-permute-start.2 = (bf16[128,2048]{1,0:T(8,128)(2,1)}, bf16[128,2048]{1,0:T(8,128)(2,1)S(1)}, u32[]{:S(2)}, u32[]{:S(2)}) collective-permute-start(bf16[128,2048]{1,0:T(8,128)(2,1)} %tokens.1), channel_id=1, source_target_pairs={{0,24},{1,25},{2,26},{3,27},{4,28},{5,29},{6,30},{7,31},{8,0},{9,1... | collective-permute-start | bytes 1572872 | tf_op jit(solution)/shard_map/ppermute | solution.py:41
  4.9 31.9 %collective-permute-start.1 = (bf16[128,2048]{1,0:T(8,128)(2,1)}, bf16[128,2048]{1,0:T(8,128)(2,1)S(1)}, u32[]{:S(2)}, u32[]{:S(2)}) collective-permute-start(bf16[128,2048]{1,0:T(8,128)(2,1)} %tokens.1), channel_id=1, source_target_pairs={{0,16},{1,17},{2,18},{3,19},{4,20},{5,21},{6,22},{7,23},{8,24},{9,... | collective-permute-start | bytes 1572872 | tf_op jit(solution)/shard_map/ppermute | solution.py:41
  29.6 37.4 %collective-permute-start.23 = (bf16[128,2048]{1,0:T(8,128)(2,1)}, bf16[128,2048]{1,0:T(8,128)(2,1)S(1)}, u32[]{:S(2)}, u32[]{:S(2)}) collective-permute-start(bf16[128,2048]{1,0:T(8,128)(2,1)} %cot.1), channel_id=1, source_target_pairs={{0,2},{1,3},{2,4},{3,5},{4,6},{5,7},{6,0},{7,1},{8,10},{9,11},{10,... | collective-permute-start | bytes 1572872 | tf_op jit(solution)/shard_map/ppermute | solution.py:41
  33.2 33.8 %collective-permute-start.25 = (bf16[128,2048]{1,0:T(8,128)(2,1)}, bf16[128,2048]{1,0:T(8,128)(2,1)S(1)}, u32[]{:S(2)}, u32[]{:S(2)}) collective-permute-start(bf16[128,2048]{1,0:T(8,128)(2,1)} %cot.1), channel_id=1, source_target_pairs={{0,6},{1,7},{2,0},{3,1},{4,2},{5,3},{6,4},{7,5},{8,14},{9,15},{10,... | collective-permute-start | bytes 1572872 | tf_op jit(solution)/shard_map/ppermute | solution.py:41
  36.0 34.3 %collective-permute-start.24 = (bf16[128,2048]{1,0:T(8,128)(2,1)}, bf16[128,2048]{1,0:T(8,128)(2,1)S(1)}, u32[]{:S(2)}, u32[]{:S(2)}) collective-permute-start(bf16[128,2048]{1,0:T(8,128)(2,1)} %cot.1), channel_id=1, source_target_pairs={{0,4},{1,5},{2,6},{3,7},{4,0},{5,1},{6,2},{7,3},{8,12},{9,13},{10,... | collective-permute-start | bytes 1572872 | tf_op jit(solution)/shard_map/ppermute | solution.py:41
  39.6 31.1 %collective-permute-start.6 = (bf16[128,2048]{1,0:T(8,128)(2,1)S(1)}, bf16[128,2048]{1,0:T(8,128)(2,1)S(1)}, u32[]{:S(2)}, u32[]{:S(2)}) collective-permute-start(bf16[128,2048]{1,0:T(8,128)(2,1)S(1)} %get-tuple-element.81), channel_id=1, source_target_pairs={{0,1},{1,0},{2,3},{3,2},{4,5},{5,4},{6,7},{7,6},{8,9},{9,8},{10,11... | collective-permute-start | bytes 1572872 | tf_op jit(solution)/shard_map/ppermute | solution.py:41
  67.0 37.7 %collective-permute-start.10 = (bf16[128,2048]{1,0:T(8,128)(2,1)S(1)}, bf16[128,2048]{1,0:T(8,128)(2,1)S(1)}, u32[]{:S(2)}, u32[]{:S(2)}) collective-permute-start(bf16[128,2048]{1,0:T(8,128)(2,1)S(1)} %get-tuple-element.86), channel_id=1, source_target_pairs={{0,6},{1,7},{2,0},{3,1},{4,2},{5,3},{6,4},{7,5},{8,14},{9,15},{10,... | collective-permute-start | bytes 1572872 | tf_op jit(solution)/shard_map/ppermute | solution.py:41
  70.3 34.8 %collective-permute-start.14 = (bf16[128,2048]{1,0:T(8,128)(2,1)S(1)}, bf16[128,2048]{1,0:T(8,128)(2,1)S(1)}, u32[]{:S(2)}, u32[]{:S(2)}) collective-permute-start(bf16[128,2048]{1,0:T(8,128)(2,1)S(1)} %get-tuple-element.90), channel_id=1, source_target_pairs={{0,4},{1,5},{2,6},{3,7},{4,0},{5,1},{6,2},{7,3},{8,12},{9,13},{10,... | collective-permute-start | bytes 1572872 | tf_op jit(solution)/shard_map/ppermute | solution.py:41
  70.7 36.7 %collective-permute-start.15 = (bf16[128,2048]{1,0:T(8,128)(2,1)S(1)}, bf16[128,2048]{1,0:T(8,128)(2,1)S(1)}, u32[]{:S(2)}, u32[]{:S(2)}) collective-permute-start(bf16[128,2048]{1,0:T(8,128)(2,1)S(1)} %get-tuple-element.91), channel_id=1, source_target_pairs={{0,5},{1,4},{2,7},{3,6},{4,1},{5,0},{6,3},{7,2},{8,13},{9,12},{10,... | collective-permute-start | bytes 1572872 | tf_op jit(solution)/shard_map/ppermute | solution.py:41
  82.4 33.2 %collective-permute-start.11 = (bf16[128,2048]{1,0:T(8,128)(2,1)S(1)}, bf16[128,2048]{1,0:T(8,128)(2,1)S(1)}, u32[]{:S(2)}, u32[]{:S(2)}) collective-permute-start(bf16[128,2048]{1,0:T(8,128)(2,1)S(1)} %get-tuple-element.87), channel_id=1, source_target_pairs={{0,7},{1,6},{2,1},{3,0},{4,3},{5,2},{6,5},{7,4},{8,15},{9,14},{10,... | collective-permute-start | bytes 1572872 | tf_op jit(solution)/shard_map/ppermute | solution.py:41
  90.0 30.0 %collective-permute-start.29 = (bf16[128,2048]{1,0:T(8,128)(2,1)S(1)}, bf16[128,2048]{1,0:T(8,128)(2,1)S(1)}, u32[]{:S(2)}, u32[]{:S(2)}) collective-permute-start(bf16[128,2048]{1,0:T(8,128)(2,1)S(1)} %get-tuple-element.101), channel_id=1, source_target_pairs={{0,16},{1,17},{2,18},{3,19},{4,20},{5,21},{6,22},{7,23},{8,24},{9,... | collective-permute-start | bytes 1572872 | tf_op jit(solution)/shard_map/ppermute | solution.py:41
  107.4 23.2 %collective-permute-start.33 = (bf16[128,2048]{1,0:T(8,128)(2,1)S(1)}, bf16[128,2048]{1,0:T(8,128)(2,1)S(1)}, u32[]{:S(2)}, u32[]{:S(2)}) collective-permute-start(bf16[128,2048]{1,0:T(8,128)(2,1)S(1)} %get-tuple-element.116), channel_id=1, source_target_pairs={{0,8},{1,9},{2,10},{3,11},{4,12},{5,13},{6,14},{7,15},{8,16},{9,17... | collective-permute-start | bytes 1572872 | tf_op jit(solution)/shard_map/ppermute | solution.py:41
  115.6 26.3 %collective-permute-start.34 = (bf16[128,2048]{1,0:T(8,128)(2,1)S(1)}, bf16[128,2048]{1,0:T(8,128)(2,1)S(1)}, u32[]{:S(2)}, u32[]{:S(2)}) collective-permute-start(bf16[128,2048]{1,0:T(8,128)(2,1)S(1)} %get-tuple-element.117), channel_id=1, source_target_pairs={{0,9},{1,8},{2,11},{3,10},{4,13},{5,12},{6,15},{7,14},{8,17},{9,16... | collective-permute-start | bytes 1572872 | tf_op jit(solution)/shard_map/ppermute | solution.py:41
  122.0 24.0 %collective-permute-start.36 = (bf16[128,2048]{1,0:T(8,128)(2,1)S(1)}, bf16[128,2048]{1,0:T(8,128)(2,1)S(1)}, u32[]{:S(2)}, u32[]{:S(2)}) collective-permute-start(bf16[128,2048]{1,0:T(8,128)(2,1)S(1)} %get-tuple-element.119), channel_id=1, source_target_pairs={{0,25},{1,24},{2,27},{3,26},{4,29},{5,28},{6,31},{7,30},{8,1},{9,0... | collective-permute-start | bytes 1572872 | tf_op jit(solution)/shard_map/ppermute | solution.py:41
  122.0 24.0 %collective-permute-start.16 = (bf16[128,2048]{1,0:T(8,128)(2,1)S(1)}, bf16[128,2048]{1,0:T(8,128)(2,1)S(1)}, u32[]{:S(2)}, u32[]{:S(2)}) collective-permute-start(bf16[128,2048]{1,0:T(8,128)(2,1)S(1)} %get-tuple-element.92), channel_id=1, source_target_pairs={{0,4},{1,5},{2,6},{3,7},{4,0},{5,1},{6,2},{7,3},{8,12},{9,13},{10,... | collective-permute-start | bytes 1572872 | tf_op jit(solution)/shard_map/ppermute | solution.py:41
  146.0 24.0 %collective-permute-start.13 = (bf16[128,2048]{1,0:T(8,128)(2,1)S(1)}, bf16[128,2048]{1,0:T(8,128)(2,1)S(1)}, u32[]{:S(2)}, u32[]{:S(2)}) collective-permute-start(bf16[128,2048]{1,0:T(8,128)(2,1)S(1)} %get-tuple-element.89), channel_id=1, source_target_pairs={{0,7},{1,6},{2,1},{3,0},{4,3},{5,2},{6,5},{7,4},{8,15},{9,14},{10,... | collective-permute-start | bytes 1572872 | tf_op jit(solution)/shard_map/ppermute | solution.py:41
  146.1 25.4 %collective-permute-start.18 = (bf16[128,2048]{1,0:T(8,128)(2,1)S(1)}, bf16[128,2048]{1,0:T(8,128)(2,1)S(1)}, u32[]{:S(2)}, u32[]{:S(2)}) collective-permute-start(bf16[128,2048]{1,0:T(8,128)(2,1)S(1)} %get-tuple-element.94), channel_id=1, source_target_pairs={{0,2},{1,3},{2,4},{3,5},{4,6},{5,7},{6,0},{7,1},{8,10},{9,11},{10,... | collective-permute-start | bytes 1572872 | tf_op jit(solution)/shard_map/ppermute | solution.py:41
  155.8 25.9 %collective-permute-start.37 = (bf16[136,2048]{1,0:T(8,128)(2,1)S(1)}, bf16[136,2048]{1,0:T(8,128)(2,1)S(1)}, u32[]{:S(2)}, u32[]{:S(2)}) collective-permute-start(bf16[136,2048]{1,0:T(8,128)(2,1)S(1)} %get-tuple-element.120), channel_id=1, source_target_pairs={{0,24},{1,25},{2,26},{3,27},{4,28},{5,29},{6,30},{7,31},{8,0},{9,1... | collective-permute-start | bytes 1671176 | tf_op jit(solution)/shard_map/ppermute | solution.py:41
  159.6 25.2 %collective-permute-start.38 = (bf16[136,2048]{1,0:T(8,128)(2,1)S(1)}, bf16[136,2048]{1,0:T(8,128)(2,1)S(1)}, u32[]{:S(2)}, u32[]{:S(2)}) collective-permute-start(bf16[136,2048]{1,0:T(8,128)(2,1)S(1)} %get-tuple-element.121), channel_id=1, source_target_pairs={{0,25},{1,24},{2,27},{3,26},{4,29},{5,28},{6,31},{7,30},{8,1},{9,0... | collective-permute-start | bytes 1671176 | tf_op jit(solution)/shard_map/ppermute | solution.py:41
  171.4 26.9 %collective-permute-start.42 = (bf16[136,2048]{1,0:T(8,128)(2,1)S(1)}, bf16[136,2048]{1,0:T(8,128)(2,1)S(1)}, u32[]{:S(2)}, u32[]{:S(2)}) collective-permute-start(bf16[136,2048]{1,0:T(8,128)(2,1)S(1)} %get-tuple-element.125), channel_id=1, source_target_pairs={{0,9},{1,8},{2,11},{3,10},{4,13},{5,12},{6,15},{7,14},{8,17},{9,16... | collective-permute-start | bytes 1671176 | tf_op jit(solution)/shard_map/ppermute | solution.py:41
  172.5 28.8 %collective-permute-start.32 = (bf16[136,2048]{1,0:T(8,128)(2,1)S(1)}, bf16[136,2048]{1,0:T(8,128)(2,1)S(1)}, u32[]{:S(2)}, u32[]{:S(2)}) collective-permute-start(bf16[136,2048]{1,0:T(8,128)(2,1)S(1)} %get-tuple-element.115), channel_id=1, source_target_pairs={{0,1},{1,0},{2,3},{3,2},{4,5},{5,4},{6,7},{7,6},{8,9},{9,8},{10,11... | collective-permute-start | bytes 1671176 | tf_op jit(solution)/shard_map/ppermute | solution.py:41
  181.7 54.3 %collective-permute-start.46 = (bf16[1408,512]{1,0:T(8,128)(2,1)S(1)}, bf16[1408,512]{1,0:T(8,128)(2,1)S(1)}, u32[]{:S(2)}, u32[]{:S(2)}) collective-permute-start(bf16[1408,512]{1,0:T(8,128)(2,1)S(1)} %get-tuple-element.137), channel_id=1, source_target_pairs={{0,96},{32,0},{64,32},{96,64},{1,97},{33,1},{65,33},{97,65},{2,98}... | collective-permute-start | bytes 4325384 | tf_op jit(solution)/shard_map/ppermute | solution.py:511
  184.8 51.2 %collective-permute-start.47 = (bf16[1408,512]{1,0:T(8,128)(2,1)S(1)}, bf16[1408,512]{1,0:T(8,128)(2,1)S(1)}, u32[]{:S(2)}, u32[]{:S(2)}) collective-permute-start(bf16[1408,512]{1,0:T(8,128)(2,1)S(1)} %get-tuple-element.138), channel_id=1, source_target_pairs={{0,32},{32,64},{64,96},{96,0},{1,33},{33,65},{65,97},{97,1},{2,34}... | collective-permute-start | bytes 4325384 | tf_op jit(solution)/shard_map/ppermute | solution.py:511
  186.7 23.3 %collective-permute-start.39 = (bf16[136,2048]{1,0:T(8,128)(2,1)S(1)}, bf16[136,2048]{1,0:T(8,128)(2,1)S(1)}, u32[]{:S(2)}, u32[]{:S(2)}) collective-permute-start(bf16[136,2048]{1,0:T(8,128)(2,1)S(1)} %get-tuple-element.122), channel_id=1, source_target_pairs={{0,16},{1,17},{2,18},{3,19},{4,20},{5,21},{6,22},{7,23},{8,24},{9,... | collective-permute-start | bytes 1671176 | tf_op jit(solution)/shard_map/ppermute | solution.py:41
  198.3 33.2 %collective-permute-start.50 = (bf16[176,2048]{1,0:T(8,128)(2,1)S(1)}, bf16[176,2048]{1,0:T(8,128)(2,1)S(1)}, u32[]{:S(2)}, u32[]{:S(2)}) collective-permute-start(bf16[176,2048]{1,0:T(8,128)(2,1)S(1)} %get-tuple-element.144), channel_id=1, source_target_pairs={{0,96},{32,0},{64,32},{96,64},{1,97},{33,1},{65,33},{97,65},{2,98}... | collective-permute-start | bytes 2162696 | tf_op jit(solution)/shard_map/ppermute | solution.py:511
  201.4 33.6 %collective-permute-start.51 = (bf16[176,2048]{1,0:T(8,128)(2,1)S(1)}, bf16[176,2048]{1,0:T(8,128)(2,1)S(1)}, u32[]{:S(2)}, u32[]{:S(2)}) collective-permute-start(bf16[176,2048]{1,0:T(8,128)(2,1)S(1)} %get-tuple-element.145), channel_id=1, source_target_pairs={{0,32},{32,64},{64,96},{96,0},{1,33},{33,65},{65,97},{97,1},{2,34}... | collective-permute-start | bytes 2162696 | tf_op jit(solution)/shard_map/ppermute | solution.py:511
  236.0 24.3 %collective-permute-start.52 = (bf16[176,1024]{1,0:T(8,128)(2,1)S(1)}, bf16[176,1024]{1,0:T(8,128)(2,1)S(1)}, u32[]{:S(2)}, u32[]{:S(2)}) collective-permute-start(bf16[176,1024]{1,0:T(8,128)(2,1)S(1)} %get-tuple-element.148), channel_id=1, source_target_pairs={{0,32},{32,64},{64,96},{96,0},{1,33},{33,65},{65,97},{97,1},{2,34}... | collective-permute-start | bytes 1081352 | tf_op jit(solution)/shard_map/ppermute | solution.py:511
  236.0 25.2 %collective-permute-start.53 = (bf16[176,1024]{1,0:T(8,128)(2,1)S(1)}, bf16[176,1024]{1,0:T(8,128)(2,1)S(1)}, u32[]{:S(2)}, u32[]{:S(2)}) collective-permute-start(bf16[176,1024]{1,0:T(8,128)(2,1)S(1)} %get-tuple-element.149), channel_id=1, source_target_pairs={{0,96},{32,0},{64,32},{96,64},{1,97},{33,1},{65,33},{97,65},{2,98}... | collective-permute-start | bytes 1081352 | tf_op jit(solution)/shard_map/ppermute | solution.py:511
  239.6 49.5 %collective-permute-start.48 = (bf16[704,512]{1,0:T(8,128)(2,1)S(1)}, bf16[704,512]{1,0:T(8,128)(2,1)S(1)}, u32[]{:S(2)}, u32[]{:S(2)}) collective-permute-start(bf16[704,512]{1,0:T(8,128)(2,1)S(1)} %get-tuple-element.141), channel_id=1, source_target_pairs={{0,32},{32,64},{64,96},{96,0},{1,33},{33,65},{65,97},{97,1},{2,34}... | collective-permute-start | bytes 2162696 | tf_op jit(solution)/shard_map/ppermute | solution.py:511
  247.9 41.2 %collective-permute-start.49 = (bf16[704,512]{1,0:T(8,128)(2,1)S(1)}, bf16[704,512]{1,0:T(8,128)(2,1)S(1)}, u32[]{:S(2)}, u32[]{:S(2)}) collective-permute-start(bf16[704,512]{1,0:T(8,128)(2,1)S(1)} %get-tuple-element.142), channel_id=1, source_target_pairs={{0,96},{32,0},{64,32},{96,64},{1,97},{33,1},{65,33},{97,65},{2,98}... | collective-permute-start | bytes 2162696 | tf_op jit(solution)/shard_map/ppermute | solution.py:511
  261.3 26.7 %collective-permute-start.45 = (bf16[136,2048]{1,0:T(8,128)(2,1)S(1)}, bf16[136,2048]{1,0:T(8,128)(2,1)S(1)}, u32[]{:S(2)}, u32[]{:S(2)}) collective-permute-start(bf16[136,2048]{1,0:T(8,128)(2,1)S(1)} %get-tuple-element.129), channel_id=1, source_target_pairs={{0,2},{1,3},{2,4},{3,5},{4,6},{5,7},{6,0},{7,1},{8,10},{9,11},{10,... | collective-permute-start | bytes 1671176 | tf_op jit(solution)/shard_map/ppermute | solution.py:41
  (28 other events, 431.4 us)
